TPU v7x, 256 devices: a whole 4x4x8 slice. The times are simulated.
256 devices in a mesh: blk: 64 (over y, z_hi, x), grp: 4 (over z_lo, core).
Axes of the slice: x: 4, y: 4, z: 8 (z_hi: 4, z_lo: 2; z = z_hi * 2 + z_lo), core: 2. Of those that a mesh axis runs over, the one named last changes fastest.
Arguments:
- user_factors: float32 [262144, 128], P(('blk', 'grp')), may hold values from -1.8 to 1.8
- user_accum: float32 [262144], P(('blk', 'grp')), may hold values from 10 to 200
- friend_factors: float32 [262144, 128], P(('blk', 'grp')), may hold values from -1.8 to 1.8
- friend_accum: float32 [262144], P(('blk', 'grp')), may hold values from 10 to 200
- item_factors: float32 [32768, 128], P('blk'), may hold values from -1.8 to 1.8
- item_accum: float32 [32768], P('blk'), may hold values from 10 to 200
- rating_values: bfloat16 [2, 8192, 128, 128], P(None, ('blk', 'grp')), may hold values from -4 to 4
- rating_masks: int32 [2, 8192, 10, 128], P(None, ('blk', 'grp')), may hold values from 0 to 16383, as said below
- rating_rows: int32 [2, 8192], P(None, ('blk', 'grp')), may hold values from 0 to 7, as said below
- rating_cols: int32 [2, 8192], P(None, ('blk', 'grp')), may hold values from 0 to 3, as said below
- rating_counts: int32 [2, 256], P(None, ('blk', 'grp')), may hold values from 1 to 32, as said below
- trust_values: bfloat16 [12288, 128, 128], P(('blk', 'grp')), may hold values from 0 to 1
- trust_masks: int32 [12288, 10, 128], P(('blk', 'grp')), may hold values from 0 to 16383, as said below
- trust_rows: int32 [12288], P(('blk', 'grp')), may hold values from 0 to 7, as said below
- trust_cols: int32 [12288], P(('blk', 'grp')), may hold values from 0 to 7, as said below
- trust_counts: int32 [256], P(('blk', 'grp')), may hold values from 1 to 48, as said below
Outputs:
- user_out: float32 [262144, 128], P(('blk', 'grp'))
- user_acc_out: float32 [262144], P(('blk', 'grp'))
- friend_out: float32 [262144, 128], P(('blk', 'grp'))
- friend_acc_out: float32 [262144], P(('blk', 'grp'))
- item_out: float32 [32768, 128], P(('blk', 'grp'))
- item_acc_out: float32 [32768], P(('blk', 'grp'))
Inputs may be any that keep to these rules, and one draw needn't show every extreme that they name: `rating_rows`: in each stratum and group the listed (row, column) tile pairs of all slots are distinct. `rating_cols`: see rating_rows. `rating_counts`: slots at or past the count are ignored; in each stratum some group has all 32 slots live. `rating_masks`: bit i of word w at column c marks row 14 w + i of the tile; bits of rows at or past 128 are zero. `trust_rows`: in each group the listed (row, column) tile pairs of all slots are distinct. `trust_cols`: see trust_rows. `trust_counts`: slots at or past the count are ignored; some group has all 48 slots live. `trust_masks`: bit i of word w at column c marks row 14 w + i of the tile; bits of rows at or past 128 are zero.
All inputs are finite; a program needn't handle non-finite values.
Results may differ from a plain program's by a relative error of at most 0.005.
Values may be sent and summed in bfloat16 or wider, within the bound.
No kernel may reach another device: no remote copies, remote signals or barrier semaphores. Data moves between devices by JAX's collectives and lax.ppermute only.
A program may use at most 64 MiB of HBM per device.

v0:
```python
import jax
import jax.numpy as jnp
from jax import lax
from jax.experimental import pallas as pl
from jax.experimental.pallas import tpu as pltpu
from jax.sharding import PartitionSpec as P

learn_rate = 0.3
shrinkage = 0.02
T = 128
WORD_BITS = 14
UNSEEN = 2.0**100
SEEN_BELOW = 2.0**90
bf16 = jnp.bfloat16
f32 = jnp.float32
HBM = pl.BlockSpec(memory_space=pl.ANY)
VM = pl.BlockSpec(memory_space=pltpu.VMEM)
SM = pl.BlockSpec(memory_space=pltpu.SMEM)


def shape(dims, dtype):
    return jax.ShapeDtypeStruct(dims, dtype)


def matmul(a, b, ca, cb):
    return lax.dot_general(a, b, (((ca,), (cb,)), ((), ())), preferred_element_type=f32)


def tile(index):
    return slice(index * T, (index + 1) * T)


def call(body, ins, outs, scratch, flops, moved, name):
    return pl.pallas_call(
        body,
        in_specs=ins,
        out_specs=[VM] * len(outs),
        out_shape=outs,
        scratch_shapes=scratch,
        cost_estimate=pl.CostEstimate(flops=flops, bytes_accessed=moved, transcendentals=0),
        name=name,
    )


def bit_patterns():
    rows = lax.broadcasted_iota(jnp.int32, (8, T), 0)
    found = {}
    for k in range(T // 8):
        first = (8 * k) % WORD_BITS
        if first not in found:
            bit = first + rows
            second = bit >= WORD_BITS
            found[first] = (
                jnp.left_shift(1, jnp.where(second, bit - WORD_BITS, bit)),
                second if first > WORD_BITS - 8 else None,
            )
    return found


def observed(patterns, words, slot, k2):
    halves = []
    for k in (2 * k2, 2 * k2 + 1):
        w = 8 * k // WORD_BITS
        bits, second = patterns[8 * k % WORD_BITS]
        word = jnp.broadcast_to(words[w, pl.ds(slot, 1), :], (8, T))
        if second is not None:
            later = jnp.broadcast_to(words[w + 1, pl.ds(slot, 1), :], (8, T))
            word = jnp.where(second, later, word)
        halves.append((word & bits) != 0)
    return jnp.concatenate(halves, axis=0)


def invert_slots(place_of, live, slots, places, spare):
    @pl.loop(0, places)
    def _(t):
        slots[t] = spare

    @pl.loop(0, live)
    def _(q):
        slots[place_of(q)] = q


def column_of(core, j):
    return 2 * (j % 2) + (core if j < 2 else 1 - core)


def zero_spare(words, slot_total):
    words[:, slot_total:, :] = jnp.zeros((words.shape[0], words.shape[1] - slot_total, T), jnp.int32)


def first_stratum(
    rows, cols, counts, user_hbm, item_hbm, acc_hbm, friend_hbm, vals_hbm, masks_hbm,
    own_sum, other_sum, own_resid, other_resid, item_out, friend_low,
    user, item, acc, friend, vals, words, slots, right, sems,
):
    slot_total = vals_hbm.shape[1]
    core = lax.axis_index("grp") % 2
    sources = [
        (vals_hbm.at[0], vals.at[pl.ds(0, slot_total)]),
        (masks_hbm.at[0], words.at[:, pl.ds(0, slot_total), :]),
        (user_hbm, user),
        (item_hbm, item),
        (acc_hbm, acc),
        (friend_hbm, friend),
    ]
    copies = [pltpu.make_async_copy(a, b, sems.at[i]) for i, (a, b) in enumerate(sources)]
    for copy in copies:
        copy.start()
    invert_slots(lambda q: rows[0, q] * 4 + cols[0, q], counts[0, 0], slots, 32, slot_total)
    zero_spare(words, slot_total)
    patterns = bit_patterns()
    copies[3].wait()
    for j in range(4):
        column = column_of(core, j)
        rows_f32 = item[pl.ds(pl.multiple_of(column * T, T), T), :]
        right[tile(j), :] = rows_f32.astype(bf16)
        if j < 2:
            item_out[tile(j), :] = rows_f32
    copies[4].wait()
    item_out[2 * T : 2 * T + 8, :] = jnp.zeros((8, T), f32)
    for j in range(2):
        item_out[2 * T + j : 2 * T + j + 1, :] = acc[pl.ds(column_of(core, j), 1), :]
    for i in (2, 1, 0):
        copies[i].wait()
    user_low = user[...].astype(bf16)
    for r in range(8):
        predict = matmul(user_low[tile(r), :], right[...], 1, 1)
        for j in range(4):
            slot = slots[r * 4 + column_of(core, j)]
            out = own_resid if j < 2 else other_resid
            for k2 in range(T // 16):
                part = slice(16 * k2, 16 * k2 + 16)
                seen = observed(patterns, words, slot, k2)
                diff = vals[slot, part, :].astype(f32) - predict[part, tile(j)]
                out[r * T + 16 * k2 : r * T + 16 * k2 + 16, tile(j % 2)] = jnp.where(seen, diff, 0.0).astype(bf16)
    own_sum[...] = matmul(user_low, own_resid[...], 0, 0)
    other_sum[...] = matmul(user_low, other_resid[...], 0, 0).astype(bf16)
    copies[5].wait()
    friend_low[...] = friend[...].astype(bf16)


def chip_sum(own_sum, arrived, out):
    out[...] = (own_sum[...] + arrived[...].astype(f32)).astype(bf16)


def eye_mask():
    return lax.broadcasted_iota(jnp.int32, (T, T), 0) == lax.broadcasted_iota(jnp.int32, (T, T), 1)


def update_rows(eye, factor, acc_row, prod):
    grad = shrinkage * factor - prod
    spread = jnp.where(eye, jnp.broadcast_to(acc_row, (T, T)), 0.0)
    acc = jnp.sum(grad * grad * (1.0 / T) + spread, axis=1, keepdims=True)
    new = factor - grad * (learn_rate * lax.rsqrt(acc))
    acc_out = jnp.sum(jnp.where(eye, jnp.broadcast_to(acc, (T, T)), 0.0), axis=0, keepdims=True)
    return new, acc_out


def first_users(own_resid, other_resid, user, item, acc, user_mid, acc_mid, user_low):
    core = lax.axis_index("grp") % 2
    eye = eye_mask()
    halves = []
    for first in (0, 2):
        parts = [item[pl.ds(pl.multiple_of(column_of(core, j) * T, T), T), :] for j in (first, first + 1)]
        halves.append(jnp.concatenate(parts, axis=0).astype(bf16))
    prod = matmul(own_resid[...], halves[0], 1, 0) + matmul(other_resid[...], halves[1], 1, 0)
    for r in range(8):
        new, acc_out = update_rows(eye, user[tile(r), :], acc[r : r + 1, :], prod[tile(r), :])
        user_mid[tile(r), :] = new
        user_low[tile(r), :] = new.astype(bf16)
        acc_mid[r : r + 1, :] = acc_out


def place_tiles(
    rows, cols, counts, trust_rows, trust_cols, trust_count, vals_hbm, masks_hbm, trust_hbm, trust_masks_hbm,
    placed, trust_placed, vals, words, trust_vals, trust_words, slots, sems,
):
    core = lax.axis_index("grp") % 2
    rate_total, trust_total = vals_hbm.shape[1], trust_hbm.shape[0]
    sources = [
        (vals_hbm.at[1], vals.at[pl.ds(0, rate_total)]),
        (masks_hbm.at[1], words.at[:, pl.ds(0, rate_total), :]),
        (trust_hbm, trust_vals.at[pl.ds(0, trust_total)]),
        (trust_masks_hbm, trust_words.at[:, pl.ds(0, trust_total), :]),
    ]
    copies = [pltpu.make_async_copy(a, b, sems.at[i]) for i, (a, b) in enumerate(sources)]
    for copy in copies:
        copy.start()
    zero_spare(words, rate_total)
    zero_spare(trust_words, trust_total)
    patterns = bit_patterns()
    invert_slots(lambda q: rows[1, q] * 4 + cols[1, q], counts[1, 0], slots, 32, rate_total)
    copies[0].wait()
    copies[1].wait()

    def place(slot, values, packed, out, r, c):
        for k2 in range(T // 16):
            seen = observed(patterns, packed, slot, k2)
            value = jnp.where(seen, values[slot, 16 * k2 : 16 * k2 + 16, :].astype(f32), UNSEEN)
            out[pl.ds(pl.multiple_of(r * T + 16 * k2, 16), 16), tile(c)] = value.astype(bf16)

    @pl.loop(0, 8)
    def _(r):
        for j in range(4):
            place(slots[r * 4 + column_of(core, j)], vals, words, placed, r, j)

    invert_slots(lambda q: trust_rows[q] * 8 + trust_cols[q], trust_count[0], slots, 64, trust_total)
    copies[2].wait()
    copies[3].wait()

    @pl.loop(0, 8)
    def _(r):
        for c in range(8):
            place(slots[r * 8 + c], trust_vals, trust_words, trust_placed, r, c)


def items_arrive(first, second, item_prev, item_mid, acc_mid, item_low):
    eye = eye_mask()
    total = first[...].astype(f32) + second[...].astype(f32)
    for j in range(2):
        acc_row = item_prev[2 * T + j : 2 * T + j + 1, :]
        new, acc_out = update_rows(eye, item_prev[tile(j), :], acc_row, total[:, tile(j)].T)
        item_mid[tile(j), :] = new
        item_low[tile(j), :] = new.astype(bf16)
        acc_mid[j : j + 1, :] = acc_out


def residuals(left, right, placed, column, out):
    count = right.shape[0] // T
    for r in range(8):
        predict = matmul(left[tile(r), :], right[...], 1, 1)
        for j in range(count):
            value = placed[tile(r), tile(column + j)].astype(f32)
            diff = jnp.where(value < SEEN_BELOW, value - predict[:, tile(j)], 0.0)
            out[tile(r), tile(j)] = diff.astype(bf16)


def own_columns(user_low, own_low, placed, own_resid):
    residuals(user_low, own_low, placed, 0, own_resid)


def second_stratum(
    user_low, own_low, other_low, placed, own_resid, user_mid, acc_mid, far_low, trust_placed,
    other_resid, user_rated, acc_rated, rated_low, trust_resid, friend_sum,
):
    eye = eye_mask()
    residuals(user_low, other_low, placed, 2, other_resid)
    prod = matmul(own_resid[...], own_low[...], 1, 0) + matmul(other_resid[...], other_low[...], 1, 0)
    for r in range(8):
        new, acc_out = update_rows(eye, user_mid[tile(r), :], acc_mid[r : r + 1, :], prod[tile(r), :])
        user_rated[tile(r), :] = new
        rated_low[tile(r), :] = new.astype(bf16)
        acc_rated[r : r + 1, :] = acc_out
    residuals(rated_low, far_low.at[pl.ds(0, 4 * T)], trust_placed, 0, trust_resid)
    friend_sum[...] = matmul(rated_low[...], trust_resid[...], 0, 0).astype(bf16)


def second_half(rated_low, far_low, trust_placed, trust_resid, friend_sum):
    residuals(rated_low, far_low.at[pl.ds(4 * T, 4 * T)], trust_placed, 4, trust_resid)
    friend_sum[...] = matmul(rated_low[...], trust_resid[...], 0, 0).astype(bf16)


def item_products(user_low, own_resid, other_resid, mine, core_part, chip_part, across_part):
    near = lax.axis_index("grp") // 2
    own = matmul(user_low[...], own_resid[...], 0, 0)
    other = matmul(user_low[...], other_resid[...], 0, 0)
    flip = near == 1
    mine[...] = jnp.where(flip, own[:, T:], own[:, :T])
    chip_part[...] = jnp.where(flip, own[:, :T], own[:, T:])
    core_part[...] = jnp.where(flip, other[:, T:], other[:, :T])
    across_part[...] = jnp.where(flip, other[:, :T], other[:, T:])


def last_users(first_resid, second_resid, far_low, user_rated, acc_rated, user_out, acc_out):
    eye = eye_mask()
    half = 4 * T
    prod = matmul(first_resid[...], far_low[:half, :], 1, 0) + matmul(second_resid[...], far_low[half:, :], 1, 0)
    for r in range(8):
        new, acc = update_rows(eye, user_rated[tile(r), :], acc_rated[r : r + 1, :], prod[tile(r), :])
        user_out[tile(r), :] = new
        acc_out[r : r + 1, :] = acc


def last_items(mine, core_part, chip_part, across_part, item_mid, acc_mid, item_out, acc_out):
    near = lax.axis_index("grp") // 2
    total = mine[...] + core_part[...] + chip_part[...] + across_part[...]
    factor = item_mid[pl.ds(pl.multiple_of(near * T, T), T), :]
    new, acc = update_rows(eye_mask(), factor, acc_mid[pl.ds(near, 1), :], total.T)
    item_out[...] = new
    acc_out[...] = acc


def last_friends(first, second, friend, acc, friend_out, acc_out):
    eye = eye_mask()
    for r in range(8):
        arrived = first if r < 4 else second
        prod = arrived[:, tile(r % 4)].astype(f32).T
        new, acc_row = update_rows(eye, friend[tile(r), :], acc[r : r + 1, :], prod)
        friend_out[tile(r), :] = new
        acc_out[r : r + 1, :] = acc_row


def local(
    user_factors, user_accum, friend_factors, friend_accum, item_factors, item_accum,
    rating_values, rating_masks, rating_rows, rating_cols, rating_counts,
    trust_values, trust_masks, trust_rows, trust_cols, trust_counts,
):
    blocks, groups = lax.axis_size("blk"), lax.axis_size("grp")
    axes = ("blk", "grp")

    def send(value, to):
        route = []
        for b in range(blocks):
            for g in range(groups):
                tb, tg = to(b, g)
                route.append((b * groups + g, tb % blocks * groups + tg))
        return lax.ppermute(value, axes, route)

    words_of = rating_masks.transpose(0, 2, 1, 3)
    trust_words_of = trust_masks.transpose(1, 0, 2)
    user_acc = user_accum.reshape(8, T)
    friend_acc = friend_accum.reshape(8, T)
    item_acc = item_accum.reshape(4, T)

    own_sum, other_sum, own_resid, other_resid, item_send, friend_low = call(
        first_stratum,
        [SM, SM, SM] + [HBM] * 6,
        [
            shape((T, 2 * T), f32), shape((T, 2 * T), bf16), shape((8 * T, 2 * T), bf16), shape((8 * T, 2 * T), bf16),
            shape((2 * T + 8, T), f32), shape((8 * T, T), bf16),
        ],
        [
            pltpu.VMEM((8 * T, T), f32), pltpu.VMEM((4 * T, T), f32), pltpu.VMEM((4, T), f32), pltpu.VMEM((8 * T, T), f32),
            pltpu.VMEM((33, T, T), bf16), pltpu.VMEM((10, 40, T), jnp.int32), pltpu.SMEM((32,), jnp.int32),
            pltpu.VMEM((4 * T, T), bf16), pltpu.SemaphoreType.DMA((6,)),
        ],
        270_000_000, 3_000_000, "first_stratum",
    )(rating_rows, rating_cols, rating_counts, user_factors, item_factors, item_acc, friend_factors, rating_values, words_of)

    other_arrived = send(other_sum, lambda b, g: (b, g ^ 1))
    item_prev = send(item_send, lambda b, g: (b + 1, g))
    chip = call(chip_sum, [VM, VM], [shape((T, 2 * T), bf16)], [], 100_000, 300_000, "chip_sum")(own_sum, other_arrived)[0]
    near_sum = send(chip, lambda b, g: (b + 1, g))
    cross_sum = send(chip, lambda b, g: (b + 1, g ^ 2))
    half_bit = blocks // 2
    far_low = send(friend_low, lambda b, g: (b ^ half_bit, g))

    user_mid, acc_mid, user_low = call(
        first_users,
        [VM] * 5,
        [shape((8 * T, T), f32), shape((8, T), f32), shape((8 * T, T), bf16)],
        [], 140_000_000, 3_000_000, "first_users",
    )(own_resid, other_resid, user_factors, item_factors, user_acc)
    placed, trust_placed = call(
        place_tiles,
        [SM] * 6 + [HBM] * 4,
        [shape((8 * T, 4 * T), bf16), shape((8 * T, 8 * T), bf16)],
        [
            pltpu.VMEM((33, T, T), bf16), pltpu.VMEM((10, 40, T), jnp.int32),
            pltpu.VMEM((49, T, T), bf16), pltpu.VMEM((10, 56, T), jnp.int32),
            pltpu.SMEM((64,), jnp.int32), pltpu.SemaphoreType.DMA((4,)),
        ],
        20_000_000, 6_000_000, "place_tiles",
    )(rating_rows, rating_cols, rating_counts, trust_rows, trust_cols, trust_counts, rating_values, words_of, trust_values, trust_words_of)

    item_mid, item_acc_mid, own_low = call(
        items_arrive,
        [VM] * 3,
        [shape((2 * T, T), f32), shape((2, T), f32), shape((2 * T, T), bf16)],
        [], 1_000_000, 500_000, "items_arrive",
    )(near_sum, cross_sum, item_prev)
    other_low = send(own_low, lambda b, g: (b, g ^ 1))
    own_resid = call(
        own_columns, [VM] * 3, [shape((8 * T, 2 * T), bf16)], [], 67_000_000, 1_000_000, "own_columns"
    )(user_low, own_low, placed)[0]
    other_resid, user_rated, acc_rated, rated_low, trust_a, friend_a = call(
        second_stratum,
        [VM] * 9,
        [
            shape((8 * T, 2 * T), bf16), shape((8 * T, T), f32), shape((8, T), f32), shape((8 * T, T), bf16),
            shape((8 * T, 4 * T), bf16), shape((T, 4 * T), bf16),
        ],
        [], 400_000_000, 6_000_000, "second_stratum",
    )(user_low, own_low, other_low, placed, own_resid, user_mid, acc_mid, far_low, trust_placed)
    home_a = send(friend_a, lambda b, g: (b ^ half_bit, g))
    trust_b, friend_b = call(
        second_half,
        [VM] * 3,
        [shape((8 * T, 4 * T), bf16), shape((T, 4 * T), bf16)],
        [], 270_000_000, 3_000_000, "second_half",
    )(rated_low, far_low, trust_placed)
    home_b = send(friend_b, lambda b, g: (b ^ half_bit, g))
    mine, core_part, chip_part, across_part = call(
        item_products,
        [VM] * 3,
        [shape((T, T), f32)] * 4,
        [], 140_000_000, 1_500_000, "item_products",
    )(user_low, own_resid, other_resid)
    core_part = send(core_part, lambda b, g: (b, g ^ 1))
    chip_part = send(chip_part, lambda b, g: (b, g ^ 2))
    across_part = send(across_part, lambda b, g: (b, g ^ 3))
    user_out, user_acc_out = call(
        last_users,
        [VM] * 5,
        [shape((8 * T, T), f32), shape((8, T), f32)],
        [], 270_000_000, 4_000_000, "last_users",
    )(trust_a, trust_b, far_low, user_rated, acc_rated)
    item_out, item_acc_out = call(
        last_items, [VM] * 6, [shape((T, T), f32), shape((1, T), f32)], [], 1_000_000, 400_000, "last_items"
    )(mine, core_part, chip_part, across_part, item_mid, item_acc_mid)
    friend_out, friend_acc_out = call(
        last_friends,
        [VM] * 4,
        [shape((8 * T, T), f32), shape((8, T), f32)],
        [], 4_000_000, 1_500_000, "last_friends",
    )(home_a, home_b, friend_factors, friend_acc)
    return (
        user_out,
        user_acc_out.reshape(8 * T),
        friend_out,
        friend_acc_out.reshape(8 * T),
        item_out,
        item_acc_out.reshape(T),
    )


def solution(mesh):
    both = ("blk", "grp")
    return jax.shard_map(
        local,
        mesh=mesh,
        in_specs=(
            P(both, None), P(both), P(both, None), P(both), P("blk", None), P("blk"),
            P(None, both, None, None), P(None, both, None, None), P(None, both), P(None, both), P(None, both),
            P(both, None, None), P(both, None, None), P(both), P(both), P(both),
        ),
        out_specs=(P(both, None), P(both), P(both, None), P(both), P(both, None), P(both)),
        check_vma=False,
    )
```

profile of v0, /device:TPU:1, one launch (start us, length us, event | category | flops | bytes accessed | tf_op | source)
XLA Modules:
  0.0 72.9 jit_solution(9197973161705620565)
XLA Ops:
  0.6 1.3 %copy.22.counts = s32[2,1]{1,0:T(2,128)} copy(s32[2,1]{0,1:T(1,128)} %param.26) | data formatting | bytes 16 | tf_op args[10]
  1.9 4.3 %first_stratum.1 = (f32[128,256]{1,0:T(8,128)}, bf16[128,256]{1,0:T(8,128)(2,1)}, bf16[1024,256]{1,0:T(8,128)(2,1)}, bf16[1024,256]{1,0:T(8,128)(2,1)}, f32[264,128]{1,0:T(8,128)}, /*index=5*/bf16[1024,128]{1,0:T(8,128)(2,1)}) custom-call(s32[2,32]{1,0:T(2,128)} %rows.3, s32[2,32]{1,0:T(2,128)} %cols.3, s32[2,1]{1,0:T(2,128)} %copy.22.counts, ...), custom_call_target="tpu_custom_call" | custom-call | flops 270000000 | bytes 3000000 | tf_op jit(solution)/shard_map/first_stratum/pallas_call | solution.py:325
  6.3 3.8 %collective-permute-start.5 = (bf16[1024,128]{1,0:T(8,128)(2,1)}, bf16[1024,128]{1,0:T(8,128)(2,1)S(1)}, u32[]{:S(2)}, u32[]{:S(2)}) collective-permute-start(bf16[1024,128]{1,0:T(8,128)(2,1)} %get-tuple-element.48), channel_id=1, source_target_pairs={{0,128},{1,129},{2,130},{3,131},{4,132},{5,133},{6,134},{7,135},{8... | collective-permute-start | bytes 786440 | tf_op jit(solution)/shard_map/ppermute | solution.py:317
  10.1 1.2 %collective-permute-start.3 = (f32[264,128]{1,0:T(8,128)}, f32[264,128]{1,0:T(8,128)S(1)}, u32[]{:S(2)}, u32[]{:S(2)}) collective-permute-start(f32[264,128]{1,0:T(8,128)} %get-tuple-element.43), channel_id=1, source_target_pairs={{0,4},{1,5},{2,6},{3,7},{4,8},{5,9},{6,10},{7,11},{8,12},{9,13},{1... | collective-permute-start | bytes 405512 | tf_op jit(solution)/shard_map/ppermute | solution.py:317
  11.3 1.2 %collective-permute-start = (bf16[128,256]{1,0:T(8,128)(2,1)}, bf16[128,256]{1,0:T(8,128)(2,1)S(1)}, u32[]{:S(2)}, u32[]{:S(2)}) collective-permute-start(bf16[128,256]{1,0:T(8,128)(2,1)} %get-tuple-element.42), channel_id=1, source_target_pairs={{0,1},{1,0},{2,3},{3,2},{4,5},{5,4},{6,7},{7,6},{8,9},{9,8},{10,11... | collective-permute-start | bytes 196616 | tf_op jit(solution)/shard_map/ppermute | solution.py:317
  12.5 1.1 %collective-permute-done.arrived = bf16[128,256]{1,0:T(8,128)(2,1)S(1)} collective-permute-done((bf16[128,256]{1,0:T(8,128)(2,1)}, bf16[128,256]{1,0:T(8,128)(2,1)S(1)}, u32[]{:S(2)}, u32[]{:S(2)}) %collective-permute-start) | collective-permute-done | bytes 65568 | tf_op jit(solution)/shard_map/ppermute | solution.py:317
  14.3 1.6 %chip_sum.1 = bf16[128,256]{1,0:T(8,128)(2,1)} custom-call(f32[128,256]{1,0:T(8,128)} %get-tuple-element.41.own_sum, bf16[128,256]{1,0:T(8,128)(2,1)} %copy-done.10), custom_call_target="tpu_custom_call" | custom-call | flops 100000 | bytes 300000 | tf_op jit(solution)/shard_map/chip_sum/pallas_call | solution.py:342
  15.8 2.6 %collective-permute-start.2 = (bf16[128,256]{1,0:T(8,128)(2,1)}, bf16[128,256]{1,0:T(8,128)(2,1)S(1)}, u32[]{:S(2)}, u32[]{:S(2)}) collective-permute-start(bf16[128,256]{1,0:T(8,128)(2,1)} %chip_sum.1), channel_id=1, source_target_pairs={{0,6},{1,7},{2,4},{3,5},{4,10},{5,11},{6,8},{7,9},{8,14},{9,15},{1... | collective-permute-start | bytes 196616 | tf_op jit(solution)/shard_map/ppermute | solution.py:317
  18.4 0.9 %collective-permute-start.1 = (bf16[128,256]{1,0:T(8,128)(2,1)}, bf16[128,256]{1,0:T(8,128)(2,1)S(1)}, u32[]{:S(2)}, u32[]{:S(2)}) collective-permute-start(bf16[128,256]{1,0:T(8,128)(2,1)} %chip_sum.1), channel_id=1, source_target_pairs={{0,4},{1,5},{2,6},{3,7},{4,8},{5,9},{6,10},{7,11},{8,12},{9,13},{1... | collective-permute-start | bytes 196616 | tf_op jit(solution)/shard_map/ppermute | solution.py:317
  19.3 7.1 %collective-permute-done.2.second = bf16[128,256]{1,0:T(8,128)(2,1)S(1)} collective-permute-done((bf16[128,256]{1,0:T(8,128)(2,1)}, bf16[128,256]{1,0:T(8,128)(2,1)S(1)}, u32[]{:S(2)}, u32[]{:S(2)}) %collective-permute-start.2) | collective-permute-done | bytes 65568 | tf_op jit(solution)/shard_map/ppermute | solution.py:317
  26.4 5.0 %collective-permute-done.1.first = bf16[128,256]{1,0:T(8,128)(2,1)S(1)} collective-permute-done((bf16[128,256]{1,0:T(8,128)(2,1)}, bf16[128,256]{1,0:T(8,128)(2,1)S(1)}, u32[]{:S(2)}, u32[]{:S(2)}) %collective-permute-start.1) | collective-permute-done | bytes 65568 | tf_op jit(solution)/shard_map/ppermute | solution.py:317
  32.8 1.9 %items_arrive.1 = (f32[256,128]{1,0:T(8,128)}, f32[2,128]{1,0:T(2,128)}, bf16[256,128]{1,0:T(8,128)(2,1)}) custom-call(bf16[128,256]{1,0:T(8,128)(2,1)} %copy-done.9, bf16[128,256]{1,0:T(8,128)(2,1)} %copy-done.8, f32[264,128]{1,0:T(8,128)} %copy-done.1), custom_call_target="tpu_custom_call" | custom-call | flops 1000000 | bytes 500000 | tf_op jit(solution)/shard_map/items_arrive/pallas_call | solution.py:366
  35.8 5.9 %place_tiles.1 = (bf16[1024,512]{1,0:T(8,128)(2,1)}, bf16[1024,1024]{1,0:T(8,128)(2,1)}) custom-call(s32[2,32]{1,0:T(2,128)} %rows.3, s32[2,32]{1,0:T(2,128)} %cols.3, s32[2,1]{1,0:T(2,128)} %copy.22.counts, s32[48]{0:T(128)} %trust_rows.1, s32[48]{0:T(128)} %trust_cols.1, s32[1]{0:T(128)S(6)} %copy.24.trust_count, bf16[2,32,128,128]{3,2,1,0:T(8,128)(2,1)} %vals_hbm.3, ...), custom_call_target="tpu_custom_call" | custom-call | flops 20000000 | bytes 6000000 | tf_op jit(solution)/shard_map/place_tiles/pallas_call | solution.py:354
  41.7 2.9 %first_users.1 = (f32[1024,128]{1,0:T(8,128)}, f32[8,128]{1,0:T(8,128)}, bf16[1024,128]{1,0:T(8,128)(2,1)}) custom-call(bf16[1024,256]{1,0:T(8,128)(2,1)} %get-tuple-element.38.own_resid, bf16[1024,256]{1,0:T(8,128)(2,1)} %get-tuple-element.39.other_resid, f32[1024,128]{1,0:T(8,128)} %user.1, f32[512,128]{1,0:T(8,128)} %item.1, f32[8,128]{1,0:T(8,128)} %bitcast.11), custom_call_target="tpu_custom_call" | custom-call | flops 140000000 | bytes 3000000 | tf_op jit(solution)/shard_map/first_users/pallas_call | solution.py:348
  44.6 2.5 %own_columns.1.own_resid = bf16[1024,256]{1,0:T(8,128)(2,1)} custom-call(bf16[1024,128]{1,0:T(8,128)(2,1)} %get-tuple-element.40.user_low, bf16[256,128]{1,0:T(8,128)(2,1)} %get-tuple-element.44.own_low, bf16[1024,512]{1,0:T(8,128)(2,1)} %get-tuple-element.45.placed), custom_call_target="tpu_custom_call" | custom-call | flops 67000000 | bytes 1000000 | tf_op jit(solution)/shard_map/own_columns/pallas_call | solution.py:373
  47.8 5.0 %second_stratum.1 = (bf16[1024,256]{1,0:T(8,128)(2,1)}, f32[1024,128]{1,0:T(8,128)}, f32[8,128]{1,0:T(8,128)}, bf16[1024,128]{1,0:T(8,128)(2,1)}, bf16[1024,512]{1,0:T(8,128)(2,1)}, /*index=5*/bf16[128,512]{1,0:T(8,128)(2,1)}) custom-call(bf16[1024,128]{1,0:T(8,128)(2,1)} %get-tuple-element.40.user_low, bf16[256,128]{1,0:T(8,128)(2,1)} %get-tuple-element.44.own_low, ...), custom_call_target="tpu_custom_call" | custom-call | flops 400000000 | bytes 6000000 | tf_op jit(solution)/shard_map/second_stratum/pallas_call | solution.py:376
  52.8 3.4 %second_half.1 = (bf16[1024,512]{1,0:T(8,128)(2,1)}, bf16[128,512]{1,0:T(8,128)(2,1)}) custom-call(bf16[1024,128]{1,0:T(8,128)(2,1)} %get-tuple-element.51.rated_low, bf16[1024,128]{1,0:T(8,128)(2,1)} %copy-done, bf16[1024,1024]{1,0:T(8,128)(2,1)} %get-tuple-element.49.trust_placed), custom_call_target="tpu_custom_call" | custom-call | flops 270000000 | bytes 3000000 | tf_op jit(solution)/shard_map/second_half/pallas_call | solution.py:386
  56.1 0.7 collective-permute-start.7
  56.8 2.3 %collective-permute-start.6 = (bf16[128,512]{1,0:T(8,128)(2,1)S(1)}, bf16[128,512]{1,0:T(8,128)(2,1)S(1)}, u32[]{:S(2)}, u32[]{:S(2)}) collective-permute-start(bf16[128,512]{1,0:T(8,128)(2,1)S(1)} %copy-done.11), channel_id=1, source_target_pairs={{0,128},{1,129},{2,130},{3,131},{4,132},{5,133},{6,134},{7,135},{8... | collective-permute-start | bytes 393224 | tf_op jit(solution)/shard_map/ppermute | solution.py:317
  59.1 2.3 %item_products.1 = (f32[128,128]{1,0:T(8,128)}, f32[128,128]{1,0:T(8,128)}, f32[128,128]{1,0:T(8,128)}, f32[128,128]{1,0:T(8,128)}) custom-call(bf16[1024,128]{1,0:T(8,128)(2,1)} %get-tuple-element.40.user_low, bf16[1024,256]{1,0:T(8,128)(2,1)} %own_columns.1.own_resid, bf16[1024,256]{1,0:T(8,128)(2,1)} %get-tuple-element.61.other_resid), custom_call_target="tpu_custom_call" | custom-call | flops 140000000 | bytes 1500000 | tf_op jit(solution)/shard_map/item_products/pallas_call | solution.py:393
  61.9 1.6 %collective-permute-start.10 = (f32[128,128]{1,0:T(8,128)}, f32[128,128]{1,0:T(8,128)S(1)}, u32[]{:S(2)}, u32[]{:S(2)}) collective-permute-start(f32[128,128]{1,0:T(8,128)} %get-tuple-element.65), channel_id=1, source_target_pairs={{0,3},{1,2},{2,1},{3,0},{4,7},{5,6},{6,5},{7,4},{8,11},{9,10},{10,... | collective-permute-start | bytes 196616 | tf_op jit(solution)/shard_map/ppermute | solution.py:317
  63.5 3.3 %last_users.1 = (f32[1024,128]{1,0:T(8,128)}, f32[8,128]{1,0:T(8,128)}) custom-call(bf16[1024,512]{1,0:T(8,128)(2,1)} %get-tuple-element.50.first_resid, bf16[1024,512]{1,0:T(8,128)(2,1)} %get-tuple-element.52.second_resid, bf16[1024,128]{1,0:T(8,128)(2,1)} %copy-done, f32[1024,128]{1,0:T(8,128)} %get-tuple-element.53.user_rated, ...), custom_call_target="tpu_custom_call" | custom-call | flops 270000000 | bytes 4000000 | tf_op jit(solution)/shard_map/last_users/pallas_call | solution.py:402
  68.0 1.9 %last_items.1 = (f32[128,128]{1,0:T(8,128)}, f32[1,128]{1,0:T(1,128)}) custom-call(f32[128,128]{1,0:T(8,128)} %get-tuple-element.62.mine, f32[128,128]{1,0:T(8,128)} %copy-done.5, f32[128,128]{1,0:T(8,128)} %copy-done.6, f32[128,128]{1,0:T(8,128)} %copy-done.7, f32[256,128]{1,0:T(8,128)} %get-tuple-element.66.item_mid, f32[2,128]{1,0:T(2,128)} %get-tuple-element.67.acc_mid), custom_call_target="tpu_custom_call" | custom-call | flops 1000000 | bytes 400000 | tf_op jit(solution)/shard_map/last_items/pallas_call | solution.py:408
  70.6 2.3 %last_friends.1 = (f32[1024,128]{1,0:T(8,128)}, f32[8,128]{1,0:T(8,128)}) custom-call(bf16[128,512]{1,0:T(8,128)(2,1)} %copy-done.3, bf16[128,512]{1,0:T(8,128)(2,1)} %copy-done.2, f32[1024,128]{1,0:T(8,128)} %friend.1, f32[8,128]{1,0:T(8,128)} %bitcast.12), custom_call_target="tpu_custom_call" | custom-call | flops 4000000 | bytes 1500000 | tf_op jit(solution)/shard_map/last_friends/pallas_call | solution.py:411
  (35 shorter events, 5.5 us)
Async XLA Ops:
  6.3 40.8 %collective-permute-start.5 = (bf16[1024,128]{1,0:T(8,128)(2,1)}, bf16[1024,128]{1,0:T(8,128)(2,1)S(1)}, u32[]{:S(2)}, u32[]{:S(2)}) collective-permute-start(bf16[1024,128]{1,0:T(8,128)(2,1)} %get-tuple-element.48), channel_id=1, source_target_pairs={{0,128},{1,129},{2,130},{3,131},{4,132},{5,133},{6,134},{7,135},{8... | collective-permute-start | bytes 786440 | tf_op jit(solution)/shard_map/ppermute | solution.py:317
  10.1 21.4 %collective-permute-start.3 = (f32[264,128]{1,0:T(8,128)}, f32[264,128]{1,0:T(8,128)S(1)}, u32[]{:S(2)}, u32[]{:S(2)}) collective-permute-start(f32[264,128]{1,0:T(8,128)} %get-tuple-element.43), channel_id=1, source_target_pairs={{0,4},{1,5},{2,6},{3,7},{4,8},{5,9},{6,10},{7,11},{8,12},{9,13},{1... | collective-permute-start | bytes 405512 | tf_op jit(solution)/shard_map/ppermute | solution.py:317
  11.3 2.3 %collective-permute-start = (bf16[128,256]{1,0:T(8,128)(2,1)}, bf16[128,256]{1,0:T(8,128)(2,1)S(1)}, u32[]{:S(2)}, u32[]{:S(2)}) collective-permute-start(bf16[128,256]{1,0:T(8,128)(2,1)} %get-tuple-element.42), channel_id=1, source_target_pairs={{0,1},{1,0},{2,3},{3,2},{4,5},{5,4},{6,7},{7,6},{8,9},{9,8},{10,11... | collective-permute-start | bytes 196616 | tf_op jit(solution)/shard_map/ppermute | solution.py:317
  13.6 0.6 copy-start.10
  15.8 10.6 %collective-permute-start.2 = (bf16[128,256]{1,0:T(8,128)(2,1)}, bf16[128,256]{1,0:T(8,128)(2,1)S(1)}, u32[]{:S(2)}, u32[]{:S(2)}) collective-permute-start(bf16[128,256]{1,0:T(8,128)(2,1)} %chip_sum.1), channel_id=1, source_target_pairs={{0,6},{1,7},{2,4},{3,5},{4,10},{5,11},{6,8},{7,9},{8,14},{9,15},{1... | collective-permute-start | bytes 196616 | tf_op jit(solution)/shard_map/ppermute | solution.py:317
  18.4 13.1 %collective-permute-start.1 = (bf16[128,256]{1,0:T(8,128)(2,1)}, bf16[128,256]{1,0:T(8,128)(2,1)S(1)}, u32[]{:S(2)}, u32[]{:S(2)}) collective-permute-start(bf16[128,256]{1,0:T(8,128)(2,1)} %chip_sum.1), channel_id=1, source_target_pairs={{0,4},{1,5},{2,6},{3,7},{4,8},{5,9},{6,10},{7,11},{8,12},{9,13},{1... | collective-permute-start | bytes 196616 | tf_op jit(solution)/shard_map/ppermute | solution.py:317
  26.4 5.1 %copy-start.8 = (bf16[128,256]{1,0:T(8,128)(2,1)}, bf16[128,256]{1,0:T(8,128)(2,1)S(1)}, u32[]{:S(2)}) copy-start(bf16[128,256]{1,0:T(8,128)(2,1)S(1)} %collective-permute-done.2.second) | copy-start | bytes 196612
  31.5 0.6 copy-start.9
  32.1 0.7 copy-start.1
  34.6 12.4 %collective-permute-start.4 = (bf16[256,128]{1,0:T(8,128)(2,1)}, bf16[256,128]{1,0:T(8,128)(2,1)S(1)}, u32[]{:S(2)}, u32[]{:S(2)}) collective-permute-start(bf16[256,128]{1,0:T(8,128)(2,1)} %get-tuple-element.44.own_low), channel_id=1, source_target_pairs={{0,1},{1,0},{2,3},{3,2},{4,5},{5,4},{6,7},{7,6},{8,9},{9,8},{10,11... | collective-permute-start | bytes 196616 | tf_op jit(solution)/shard_map/ppermute | solution.py:317
  47.1 0.6 copy-start.4
  47.1 0.7 %copy-start = (bf16[1024,128]{1,0:T(8,128)(2,1)}, bf16[1024,128]{1,0:T(8,128)(2,1)S(1)}, u32[]{:S(2)}) copy-start(bf16[1024,128]{1,0:T(8,128)(2,1)S(1)} %collective-permute-done.5.far_low) | copy-start | bytes 786436
  52.8 4.1 %copy-start.11 = (bf16[128,512]{1,0:T(8,128)(2,1)S(1)}, bf16[128,512]{1,0:T(8,128)(2,1)}, u32[]{:S(2)}) copy-start(bf16[128,512]{1,0:T(8,128)(2,1)} %get-tuple-element.57) | copy-start | bytes 393220
  56.1 13.7 %collective-permute-start.7 = (bf16[128,512]{1,0:T(8,128)(2,1)}, bf16[128,512]{1,0:T(8,128)(2,1)S(1)}, u32[]{:S(2)}, u32[]{:S(2)}) collective-permute-start(bf16[128,512]{1,0:T(8,128)(2,1)} %get-tuple-element.58), channel_id=1, source_target_pairs={{0,128},{1,129},{2,130},{3,131},{4,132},{5,133},{6,134},{7,135},{8... | collective-permute-start | bytes 393224 | tf_op jit(solution)/shard_map/ppermute | solution.py:317
  56.8 13.0 %collective-permute-start.6 = (bf16[128,512]{1,0:T(8,128)(2,1)S(1)}, bf16[128,512]{1,0:T(8,128)(2,1)S(1)}, u32[]{:S(2)}, u32[]{:S(2)}) collective-permute-start(bf16[128,512]{1,0:T(8,128)(2,1)S(1)} %copy-done.11), channel_id=1, source_target_pairs={{0,128},{1,129},{2,130},{3,131},{4,132},{5,133},{6,134},{7,135},{8... | collective-permute-start | bytes 393224 | tf_op jit(solution)/shard_map/ppermute | solution.py:317
  61.4 5.5 %collective-permute-start.8 = (f32[128,128]{1,0:T(8,128)}, f32[128,128]{1,0:T(8,128)S(1)}, u32[]{:S(2)}, u32[]{:S(2)}) collective-permute-start(f32[128,128]{1,0:T(8,128)} %get-tuple-element.63), channel_id=1, source_target_pairs={{0,1},{1,0},{2,3},{3,2},{4,5},{5,4},{6,7},{7,6},{8,9},{9,8},{10,11... | collective-permute-start | bytes 196616 | tf_op jit(solution)/shard_map/ppermute | solution.py:317
  61.9 5.0 %collective-permute-start.9 = (f32[128,128]{1,0:T(8,128)}, f32[128,128]{1,0:T(8,128)S(1)}, u32[]{:S(2)}, u32[]{:S(2)}) collective-permute-start(f32[128,128]{1,0:T(8,128)} %get-tuple-element.64), channel_id=1, source_target_pairs={{0,2},{1,3},{2,0},{3,1},{4,6},{5,7},{6,4},{7,5},{8,10},{9,11},{10,... | collective-permute-start | bytes 196616 | tf_op jit(solution)/shard_map/ppermute | solution.py:317
  61.9 5.4 %collective-permute-start.10 = (f32[128,128]{1,0:T(8,128)}, f32[128,128]{1,0:T(8,128)S(1)}, u32[]{:S(2)}, u32[]{:S(2)}) collective-permute-start(f32[128,128]{1,0:T(8,128)} %get-tuple-element.65), channel_id=1, source_target_pairs={{0,3},{1,2},{2,1},{3,0},{4,7},{5,6},{6,5},{7,4},{8,11},{9,10},{10,... | collective-permute-start | bytes 196616 | tf_op jit(solution)/shard_map/ppermute | solution.py:317
  66.9 0.6 copy-start.5
  66.9 0.6 copy-start.6
  67.3 0.6 copy-start.7
  69.9 0.7 copy-start.2
  69.9 0.7 copy-start.3
where the time goes:
time: 73.4 us; the launch traced here: 72.9 us
  Pallas kernels  37.1 us (51%)
  starting transfers between devices  15.4 us (21%)
  waiting for transfers between devices  13.7 us (19%)
  local copies, waits for them, and re-layouts  5.25 us (7%)
  between operations  1.38 us (2%)
    ppermute x11, starting transfers between devices, send(): return lax.ppermute(value, axes, route)  15.4 us
    ppermute x11, waiting for transfers between devices, send(): return lax.ppermute(value, axes, route)  13.7 us
    pallas_call x1, Pallas kernels, local(): call(place_tiles, [SM] * 6 + [HBM] * 4, [shape((8 * T, 4 * T), bf16), sha...  5.88 us
    unnamed x25, local copies, waits for them, and re-layouts  5.25 us
    pallas_call x1, Pallas kernels, local(): call(second_stratum, [VM] * 9, [shape((8 * T, 2 * T), bf16), shape((8 * T...  4.96 us
    pallas_call x1, Pallas kernels, local(): call(first_stratum, [SM, SM, SM] + [HBM] * 6, [shape((T, 2 * T), f32), sh...  4.32 us
    pallas_call x1, Pallas kernels, local(): call(second_half, [VM] * 3, [shape((8 * T, 4 * T), bf16), shape((T, 4 * T...  3.35 us
    pallas_call x1, Pallas kernels, local(): call(last_users, [VM] * 5, [shape((8 * T, T), f32), shape((8, T), f32)],...  3.33 us
  transfers between devices with their start and end apart: 11, of which 4 were waited for; matrix products, arithmetic and copies ran while one was open for 0% of the time, Pallas kernels for 30%

commit v1 on v0

--- a/solution.py
+++ b/solution.py
@@ -5,17 +5,19 @@
 from jax.experimental.pallas import tpu as pltpu
 from jax.sharding import PartitionSpec as P
 
+
 learn_rate = 0.3
 shrinkage = 0.02
 T = 128
 WORD_BITS = 14
+GRANT = 24 * 2**20
 UNSEEN = 2.0**100
 SEEN_BELOW = 2.0**90
 bf16 = jnp.bfloat16
 f32 = jnp.float32
 HBM = pl.BlockSpec(memory_space=pl.ANY)
+SM = pl.BlockSpec(memory_space=pltpu.SMEM)
 VM = pl.BlockSpec(memory_space=pltpu.VMEM)
-SM = pl.BlockSpec(memory_space=pltpu.SMEM)
 
 
 def shape(dims, dtype):
@@ -30,16 +32,25 @@
     return slice(index * T, (index + 1) * T)
 
 
-def call(body, ins, outs, scratch, flops, moved, name):
-    return pl.pallas_call(
+def call(body, ins, outs, scratch, flops, moved):
+    inner = pl.pallas_call(
         body,
         in_specs=ins,
         out_specs=[VM] * len(outs),
         out_shape=outs,
         scratch_shapes=scratch,
         cost_estimate=pl.CostEstimate(flops=flops, bytes_accessed=moved, transcendentals=0),
-        name=name,
+        compiler_params=pltpu.CompilerParams(vmem_limit_bytes=GRANT),
     )
+
+    def run(*args):
+        args = [
+            pltpu.with_memory_space_constraint(arg, pltpu.HBM) if spec is HBM else arg
+            for arg, spec in zip(args, ins, strict=True)
+        ]
+        return inner(*args)
+
+    return run
 
 
 def bit_patterns():
@@ -89,9 +100,9 @@
 
 
 def first_stratum(
-    rows, cols, counts, user_hbm, item_hbm, acc_hbm, friend_hbm, vals_hbm, masks_hbm,
+    rows_hbm, cols_hbm, counts_hbm, user_hbm, item_hbm, acc_hbm, friend_hbm, vals_hbm, masks_hbm,
     own_sum, other_sum, own_resid, other_resid, item_out, friend_low,
-    user, item, acc, friend, vals, words, slots, right, sems,
+    rows, cols, counts, user, item, acc, friend, vals, words, slots, right, sems,
 ):
     slot_total = vals_hbm.shape[1]
     core = lax.axis_index("grp") % 2
@@ -102,11 +113,16 @@
         (item_hbm, item),
         (acc_hbm, acc),
         (friend_hbm, friend),
+        (rows_hbm, rows),
+        (cols_hbm, cols),
+        (counts_hbm, counts),
     ]
     copies = [pltpu.make_async_copy(a, b, sems.at[i]) for i, (a, b) in enumerate(sources)]
-    for copy in copies:
-        copy.start()
-    invert_slots(lambda q: rows[0, q] * 4 + cols[0, q], counts[0, 0], slots, 32, slot_total)
+    for i in (6, 7, 8, 0, 1, 3, 4, 2, 5):
+        copies[i].start()
+    for i in (6, 7, 8):
+        copies[i].wait()
+    invert_slots(lambda q: rows[0, q] * 4 + cols[0, q], counts[0], slots, 32, slot_total)
     zero_spare(words, slot_total)
     patterns = bit_patterns()
     copies[3].wait()
@@ -172,8 +188,9 @@
 
 
 def place_tiles(
-    rows, cols, counts, trust_rows, trust_cols, trust_count, vals_hbm, masks_hbm, trust_hbm, trust_masks_hbm,
-    placed, trust_placed, vals, words, trust_vals, trust_words, slots, sems,
+    rows_hbm, cols_hbm, counts_hbm, trust_rows_hbm, trust_cols_hbm, trust_count,
+    vals_hbm, masks_hbm, trust_hbm, trust_masks_hbm,
+    placed, trust_placed, rows, cols, counts, trust_rows, trust_cols, vals, words, trust_vals, trust_words, slots, sems,
 ):
     core = lax.axis_index("grp") % 2
     rate_total, trust_total = vals_hbm.shape[1], trust_hbm.shape[0]
@@ -182,14 +199,21 @@
         (masks_hbm.at[1], words.at[:, pl.ds(0, rate_total), :]),
         (trust_hbm, trust_vals.at[pl.ds(0, trust_total)]),
         (trust_masks_hbm, trust_words.at[:, pl.ds(0, trust_total), :]),
+        (rows_hbm, rows),
+        (cols_hbm, cols),
+        (counts_hbm, counts),
+        (trust_rows_hbm, trust_rows),
+        (trust_cols_hbm, trust_cols),
     ]
     copies = [pltpu.make_async_copy(a, b, sems.at[i]) for i, (a, b) in enumerate(sources)]
-    for copy in copies:
+    for copy in copies[4:] + copies[:4]:
         copy.start()
+    for copy in copies[4:]:
+        copy.wait()
     zero_spare(words, rate_total)
     zero_spare(trust_words, trust_total)
     patterns = bit_patterns()
-    invert_slots(lambda q: rows[1, q] * 4 + cols[1, q], counts[1, 0], slots, 32, rate_total)
+    invert_slots(lambda q: rows[1, q] * 4 + cols[1, q], counts[1], slots, 32, rate_total)
     copies[0].wait()
     copies[1].wait()
 
@@ -321,25 +345,27 @@
     user_acc = user_accum.reshape(8, T)
     friend_acc = friend_accum.reshape(8, T)
     item_acc = item_accum.reshape(4, T)
+    counts = rating_counts.reshape(2)
 
     own_sum, other_sum, own_resid, other_resid, item_send, friend_low = call(
         first_stratum,
-        [SM, SM, SM] + [HBM] * 6,
+        [HBM] * 9,
         [
             shape((T, 2 * T), f32), shape((T, 2 * T), bf16), shape((8 * T, 2 * T), bf16), shape((8 * T, 2 * T), bf16),
             shape((2 * T + 8, T), f32), shape((8 * T, T), bf16),
         ],
         [
+            pltpu.SMEM((2, 32), jnp.int32), pltpu.SMEM((2, 32), jnp.int32), pltpu.SMEM((2,), jnp.int32),
             pltpu.VMEM((8 * T, T), f32), pltpu.VMEM((4 * T, T), f32), pltpu.VMEM((4, T), f32), pltpu.VMEM((8 * T, T), f32),
             pltpu.VMEM((33, T, T), bf16), pltpu.VMEM((10, 40, T), jnp.int32), pltpu.SMEM((32,), jnp.int32),
-            pltpu.VMEM((4 * T, T), bf16), pltpu.SemaphoreType.DMA((6,)),
+            pltpu.VMEM((4 * T, T), bf16), pltpu.SemaphoreType.DMA((9,)),
         ],
-        270_000_000, 3_000_000, "first_stratum",
-    )(rating_rows, rating_cols, rating_counts, user_factors, item_factors, item_acc, friend_factors, rating_values, words_of)
+        270_000_000, 3_000_000,
+    )(rating_rows, rating_cols, counts, user_factors, item_factors, item_acc, friend_factors, rating_values, words_of)
 
     other_arrived = send(other_sum, lambda b, g: (b, g ^ 1))
     item_prev = send(item_send, lambda b, g: (b + 1, g))
-    chip = call(chip_sum, [VM, VM], [shape((T, 2 * T), bf16)], [], 100_000, 300_000, "chip_sum")(own_sum, other_arrived)[0]
+    chip = call(chip_sum, [VM, VM], [shape((T, 2 * T), bf16)], [], 100_000, 300_000)(own_sum, other_arrived)[0]
     near_sum = send(chip, lambda b, g: (b + 1, g))
     cross_sum = send(chip, lambda b, g: (b + 1, g ^ 2))
     half_bit = blocks // 2
@@ -349,29 +375,31 @@
         first_users,
         [VM] * 5,
         [shape((8 * T, T), f32), shape((8, T), f32), shape((8 * T, T), bf16)],
-        [], 140_000_000, 3_000_000, "first_users",
+        [], 140_000_000, 3_000_000,
     )(own_resid, other_resid, user_factors, item_factors, user_acc)
     placed, trust_placed = call(
         place_tiles,
-        [SM] * 6 + [HBM] * 4,
+        [HBM] * 5 + [SM] + [HBM] * 4,
         [shape((8 * T, 4 * T), bf16), shape((8 * T, 8 * T), bf16)],
         [
+            pltpu.SMEM((2, 32), jnp.int32), pltpu.SMEM((2, 32), jnp.int32), pltpu.SMEM((2,), jnp.int32),
+            pltpu.SMEM((48,), jnp.int32), pltpu.SMEM((48,), jnp.int32),
             pltpu.VMEM((33, T, T), bf16), pltpu.VMEM((10, 40, T), jnp.int32),
             pltpu.VMEM((49, T, T), bf16), pltpu.VMEM((10, 56, T), jnp.int32),
-            pltpu.SMEM((64,), jnp.int32), pltpu.SemaphoreType.DMA((4,)),
+            pltpu.SMEM((64,), jnp.int32), pltpu.SemaphoreType.DMA((9,)),
         ],
-        20_000_000, 6_000_000, "place_tiles",
-    )(rating_rows, rating_cols, rating_counts, trust_rows, trust_cols, trust_counts, rating_values, words_of, trust_values, trust_words_of)
+        20_000_000, 6_000_000,
+    )(rating_rows, rating_cols, counts, trust_rows, trust_cols, trust_counts, rating_values, words_of, trust_values, trust_words_of)
 
     item_mid, item_acc_mid, own_low = call(
         items_arrive,
         [VM] * 3,
         [shape((2 * T, T), f32), shape((2, T), f32), shape((2 * T, T), bf16)],
-        [], 1_000_000, 500_000, "items_arrive",
+        [], 1_000_000, 500_000,
     )(near_sum, cross_sum, item_prev)
     other_low = send(own_low, lambda b, g: (b, g ^ 1))
     own_resid = call(
-        own_columns, [VM] * 3, [shape((8 * T, 2 * T), bf16)], [], 67_000_000, 1_000_000, "own_columns"
+        own_columns, [VM] * 3, [shape((8 * T, 2 * T), bf16)], [], 67_000_000, 1_000_000
     )(user_low, own_low, placed)[0]
     other_resid, user_rated, acc_rated, rated_low, trust_a, friend_a = call(
         second_stratum,
@@ -380,21 +408,21 @@
             shape((8 * T, 2 * T), bf16), shape((8 * T, T), f32), shape((8, T), f32), shape((8 * T, T), bf16),
             shape((8 * T, 4 * T), bf16), shape((T, 4 * T), bf16),
         ],
-        [], 400_000_000, 6_000_000, "second_stratum",
+        [], 400_000_000, 6_000_000,
     )(user_low, own_low, other_low, placed, own_resid, user_mid, acc_mid, far_low, trust_placed)
     home_a = send(friend_a, lambda b, g: (b ^ half_bit, g))
     trust_b, friend_b = call(
         second_half,
         [VM] * 3,
         [shape((8 * T, 4 * T), bf16), shape((T, 4 * T), bf16)],
-        [], 270_000_000, 3_000_000, "second_half",
+        [], 270_000_000, 3_000_000,
     )(rated_low, far_low, trust_placed)
     home_b = send(friend_b, lambda b, g: (b ^ half_bit, g))
     mine, core_part, chip_part, across_part = call(
         item_products,
         [VM] * 3,
         [shape((T, T), f32)] * 4,
-        [], 140_000_000, 1_500_000, "item_products",
+        [], 140_000_000, 1_500_000,
     )(user_low, own_resid, other_resid)
     core_part = send(core_part, lambda b, g: (b, g ^ 1))
     chip_part = send(chip_part, lambda b, g: (b, g ^ 2))
@@ -403,16 +431,16 @@
         last_users,
         [VM] * 5,
         [shape((8 * T, T), f32), shape((8, T), f32)],
-        [], 270_000_000, 4_000_000, "last_users",
+        [], 270_000_000, 4_000_000,
     )(trust_a, trust_b, far_low, user_rated, acc_rated)
     item_out, item_acc_out = call(
-        last_items, [VM] * 6, [shape((T, T), f32), shape((1, T), f32)], [], 1_000_000, 400_000, "last_items"
+        last_items, [VM] * 6, [shape((T, T), f32), shape((1, T), f32)], [], 1_000_000, 400_000
     )(mine, core_part, chip_part, across_part, item_mid, item_acc_mid)
     friend_out, friend_acc_out = call(
         last_friends,
         [VM] * 4,
         [shape((8 * T, T), f32), shape((8, T), f32)],
-        [], 4_000_000, 1_500_000, "last_friends",
+        [], 4_000_000, 1_500_000,
     )(home_a, home_b, friend_factors, friend_acc)
     return (
         user_out,

time: 73.4 us -> 48.1 us (0.66)
  Pallas kernels: 37.1 us -> 13.7 us
  local copies, waits for them, and re-layouts: 5.25 us -> 0.03 us
  waiting for transfers between devices: 13.7 us -> 16.8 us
    pallas_call x12, Pallas kernels: 37.1 us -> 13.7 us  [run(): return inner(*args)]
    unnamed x25 -> x10, local copies, waits for them, and re-layouts: 5.25 us -> 0.03 us
    ppermute x11, waiting for transfers between devices: 13.7 us -> 16.8 us  [send(): return lax.ppermute(value, axes, route)]
  transfers between devices with their start and end apart: 11 -> 11, of which waited for: 4 -> 5; matrix products, arithmetic and copies ran while one was open for 0% -> 0% of each run, Pallas kernels for 30% -> 16%
where the time goes in v1:
time: 48.1 us; the launch traced here: 48 us
  waiting for transfers between devices  16.8 us (35%)
  starting transfers between devices  16.1 us (33%)
  Pallas kernels  13.7 us (28%)
  between operations  1.43 us (3%)
    ppermute x11, waiting for transfers between devices, send(): return lax.ppermute(value, axes, route)  16.8 us
    ppermute x11, starting transfers between devices, send(): return lax.ppermute(value, axes, route)  16.1 us
    pallas_call x12, Pallas kernels, run(): return inner(*args)  13.7 us
  transfers between devices with their start and end apart: 11, of which 5 were waited for; matrix products, arithmetic and copies ran while one was open for 0% of the time, Pallas kernels for 16%

profile of v1, /device:TPU:1, one launch (start us, length us, event | category | flops | bytes accessed | tf_op | source)
XLA Modules:
  0.0 48.0 jit_solution(13513784458435547523)
XLA Ops:
  0.6 2.5 %shard_map.199 = (f32[128,256]{1,0:T(8,128)S(1)}, bf16[128,256]{1,0:T(8,128)(2,1)S(1)}, bf16[1024,256]{1,0:T(8,128)(2,1)S(1)}, bf16[1024,256]{1,0:T(8,128)(2,1)S...) custom-call(s32[2,32]{1,0:T(2,128)} %rows_hbm.3, s32[2,32]{1,0:T(2,128)} %cols_hbm.3, s32[2]{0:T(128)} %bitcast.15, ...), custom_call_target="tpu_custom_call" | custom-call | flops 270000000 | bytes 3000000 | tf_op jit(solution)/shard_map/pallas_call | solution.py:51
  3.2 3.8 %collective-permute-start.5 = (bf16[1024,128]{1,0:T(8,128)(2,1)S(1)}, bf16[1024,128]{1,0:T(8,128)(2,1)S(1)}, u32[]{:S(2)}, u32[]{:S(2)}) collective-permute-start(bf16[1024,128]{1,0:T(8,128)(2,1)S(1)} %get-tuple-element.48), channel_id=1, source_target_pairs={{0,128},{1,129},{2,130},{3,131},{4,132},{5,133},{6,134},{7,135},{8... | collective-permute-start | bytes 786440 | tf_op jit(solution)/shard_map/ppermute | solution.py:341
  7.0 1.2 %collective-permute-start.3 = (f32[264,128]{1,0:T(8,128)S(1)}, f32[264,128]{1,0:T(8,128)S(1)}, u32[]{:S(2)}, u32[]{:S(2)}) collective-permute-start(f32[264,128]{1,0:T(8,128)S(1)} %get-tuple-element.43), channel_id=1, source_target_pairs={{0,4},{1,5},{2,6},{3,7},{4,8},{5,9},{6,10},{7,11},{8,12},{9,13},{1... | collective-permute-start | bytes 405512 | tf_op jit(solution)/shard_map/ppermute | solution.py:341
  8.2 1.2 %collective-permute-start = (bf16[128,256]{1,0:T(8,128)(2,1)S(1)}, bf16[128,256]{1,0:T(8,128)(2,1)S(1)}, u32[]{:S(2)}, u32[]{:S(2)}) collective-permute-start(bf16[128,256]{1,0:T(8,128)(2,1)S(1)} %get-tuple-element.42), channel_id=1, source_target_pairs={{0,1},{1,0},{2,3},{3,2},{4,5},{5,4},{6,7},{7,6},{8,9},{9,8},{10,11... | collective-permute-start | bytes 196616 | tf_op jit(solution)/shard_map/ppermute | solution.py:341
  9.4 0.9 %collective-permute-done.arrived = bf16[128,256]{1,0:T(8,128)(2,1)S(1)} collective-permute-done((bf16[128,256]{1,0:T(8,128)(2,1)S(1)}, bf16[128,256]{1,0:T(8,128)(2,1)S(1)}, u32[]{:S(2)}, u32[]{:S(2)}) %collective-permute-start) | collective-permute-done | bytes 65568 | tf_op jit(solution)/shard_map/ppermute | solution.py:341
  10.4 2.6 %collective-permute-start.2 = (bf16[128,256]{1,0:T(8,128)(2,1)S(1)}, bf16[128,256]{1,0:T(8,128)(2,1)S(1)}, u32[]{:S(2)}, u32[]{:S(2)}) collective-permute-start(bf16[128,256]{1,0:T(8,128)(2,1)S(1)} %shard_map.201), channel_id=1, source_target_pairs={{0,6},{1,7},{2,4},{3,5},{4,10},{5,11},{6,8},{7,9},{8,14},{9,15},{1... | collective-permute-start | bytes 196616 | tf_op jit(solution)/shard_map/ppermute | solution.py:341
  13.0 0.9 %collective-permute-start.1 = (bf16[128,256]{1,0:T(8,128)(2,1)S(1)}, bf16[128,256]{1,0:T(8,128)(2,1)S(1)}, u32[]{:S(2)}, u32[]{:S(2)}) collective-permute-start(bf16[128,256]{1,0:T(8,128)(2,1)S(1)} %shard_map.201), channel_id=1, source_target_pairs={{0,4},{1,5},{2,6},{3,7},{4,8},{5,9},{6,10},{7,11},{8,12},{9,13},{1... | collective-permute-start | bytes 196616 | tf_op jit(solution)/shard_map/ppermute | solution.py:341
  13.9 10.6 %collective-permute-done.2.second = bf16[128,256]{1,0:T(8,128)(2,1)S(1)} collective-permute-done((bf16[128,256]{1,0:T(8,128)(2,1)S(1)}, bf16[128,256]{1,0:T(8,128)(2,1)S(1)}, u32[]{:S(2)}, u32[]{:S(2)}) %collective-permute-start.2) | collective-permute-done | bytes 65568 | tf_op jit(solution)/shard_map/ppermute | solution.py:341
  24.5 2.5 %collective-permute-done.1.first = bf16[128,256]{1,0:T(8,128)(2,1)S(1)} collective-permute-done((bf16[128,256]{1,0:T(8,128)(2,1)S(1)}, bf16[128,256]{1,0:T(8,128)(2,1)S(1)}, u32[]{:S(2)}, u32[]{:S(2)}) %collective-permute-start.1) | collective-permute-done | bytes 65568 | tf_op jit(solution)/shard_map/ppermute | solution.py:341
  27.2 0.8 %collective-permute-start.4 = (bf16[256,128]{1,0:T(8,128)(2,1)S(1)}, bf16[256,128]{1,0:T(8,128)(2,1)S(1)}, u32[]{:S(2)}, u32[]{:S(2)}) collective-permute-start(bf16[256,128]{1,0:T(8,128)(2,1)S(1)} %get-tuple-element.44.own_low), channel_id=1, source_target_pairs={{0,1},{1,0},{2,3},{3,2},{4,5},{5,4},{6,7},{7,6},{8,9},{9,8},{10,11... | collective-permute-start | bytes 196616 | tf_op jit(solution)/shard_map/ppermute | solution.py:341
  28.7 3.7 %shard_map.203 = (bf16[1024,512]{1,0:T(8,128)(2,1)S(1)}, bf16[1024,1024]{1,0:T(8,128)(2,1)S(1)}) custom-call(s32[2,32]{1,0:T(2,128)} %rows_hbm.3, s32[2,32]{1,0:T(2,128)} %cols_hbm.3, s32[2]{0:T(128)} %bitcast.16, s32[48]{0:T(128)} %trust_rows_hbm.1, s32[48]{0:T(128)} %trust_cols_hbm.1, s32[1]{0:T(128)S(6)} %copy.22.trust_count, ...), custom_call_target="tpu_custom_call" | custom-call | flops 20000000 | bytes 6000000 | tf_op jit(solution)/shard_map/pallas_call | solution.py:51
  32.4 0.6 %shard_map.200 = (f32[1024,128]{1,0:T(8,128)S(1)}, f32[8,128]{1,0:T(8,128)S(1)}, bf16[1024,128]{1,0:T(8,128)(2,1)S(1)}) custom-call(bf16[1024,256]{1,0:T(8,128)(2,1)S(1)} %get-tuple-element.38.own_resid, bf16[1024,256]{1,0:T(8,128)(2,1)S(1)} %get-tuple-element.39.other_resid, f32[1024,128]{1,0:T(8,128)S(1)} %copy-done, f32[512,128]{1,0:T(8,128)S(1)} %copy-done.2, ...), custom_call_target="tpu_custom_call" | custom-call | flops 140000000 | bytes 3000000 | tf_op jit(solution)/shard_map/pallas_call | solution.py:51
  33.0 0.3 shard_map.204.own_resid
  33.4 1.7 %shard_map.205 = (bf16[1024,256]{1,0:T(8,128)(2,1)S(1)}, f32[1024,128]{1,0:T(8,128)S(1)}, f32[8,128]{1,0:T(8,128)S(1)}, bf16[1024,128]{1,0:T(8,128)(2,1)S(1)}, b...) custom-call(bf16[1024,128]{1,0:T(8,128)(2,1)S(1)} %get-tuple-element.40.user_low, ...), custom_call_target="tpu_custom_call" | custom-call | flops 400000000 | bytes 6000000 | tf_op jit(solution)/shard_map/pallas_call | solution.py:51
  35.1 0.7 %shard_map.206 = (bf16[1024,512]{1,0:T(8,128)(2,1)S(1)}, bf16[128,512]{1,0:T(8,128)(2,1)S(1)}) custom-call(bf16[1024,128]{1,0:T(8,128)(2,1)S(1)} %get-tuple-element.51.rated_low, bf16[1024,128]{1,0:T(8,128)(2,1)S(1)} %collective-permute-done.5.far_low, bf16[1024,1024]{1,0:T(8,128)(2,1)S(1)} %get-tuple-element.49.trust_placed), custom_call_target="tpu_custom_call" | custom-call | flops 270000000 | bytes 3000000 | tf_op jit(solution)/shard_map/pallas_call | solution.py:51
  35.8 0.9 %collective-permute-start.7 = (bf16[128,512]{1,0:T(8,128)(2,1)S(1)}, bf16[128,512]{1,0:T(8,128)(2,1)S(1)}, u32[]{:S(2)}, u32[]{:S(2)}) collective-permute-start(bf16[128,512]{1,0:T(8,128)(2,1)S(1)} %get-tuple-element.58), channel_id=1, source_target_pairs={{0,128},{1,129},{2,130},{3,131},{4,132},{5,133},{6,134},{7,135},{8... | collective-permute-start | bytes 393224 | tf_op jit(solution)/shard_map/ppermute | solution.py:341
  36.7 2.1 %collective-permute-start.6 = (bf16[128,512]{1,0:T(8,128)(2,1)S(1)}, bf16[128,512]{1,0:T(8,128)(2,1)S(1)}, u32[]{:S(2)}, u32[]{:S(2)}) collective-permute-start(bf16[128,512]{1,0:T(8,128)(2,1)S(1)} %get-tuple-element.57), channel_id=1, source_target_pairs={{0,128},{1,129},{2,130},{3,131},{4,132},{5,133},{6,134},{7,135},{8... | collective-permute-start | bytes 393224 | tf_op jit(solution)/shard_map/ppermute | solution.py:341
  38.9 0.3 shard_map.209
  39.2 0.6 %collective-permute-start.8 = (f32[128,128]{1,0:T(8,128)S(1)}, f32[128,128]{1,0:T(8,128)S(1)}, u32[]{:S(2)}, u32[]{:S(2)}) collective-permute-start(f32[128,128]{1,0:T(8,128)S(1)} %get-tuple-element.63), channel_id=1, source_target_pairs={{0,1},{1,0},{2,3},{3,2},{4,5},{5,4},{6,7},{7,6},{8,9},{9,8},{10,11... | collective-permute-start | bytes 196616 | tf_op jit(solution)/shard_map/ppermute | solution.py:341
  39.8 1.5 %collective-permute-start.9 = (f32[128,128]{1,0:T(8,128)S(1)}, f32[128,128]{1,0:T(8,128)S(1)}, u32[]{:S(2)}, u32[]{:S(2)}) collective-permute-start(f32[128,128]{1,0:T(8,128)S(1)} %get-tuple-element.64), channel_id=1, source_target_pairs={{0,2},{1,3},{2,0},{3,1},{4,6},{5,7},{6,4},{7,5},{8,10},{9,11},{10,... | collective-permute-start | bytes 196616 | tf_op jit(solution)/shard_map/ppermute | solution.py:341
  41.6 1.6 %shard_map.207 = (f32[1024,128]{1,0:T(8,128)}, f32[8,128]{1,0:T(8,128)}) custom-call(bf16[1024,512]{1,0:T(8,128)(2,1)S(1)} %get-tuple-element.50.first_resid, bf16[1024,512]{1,0:T(8,128)(2,1)S(1)} %get-tuple-element.52.second_resid, bf16[1024,128]{1,0:T(8,128)(2,1)S(1)} %collective-permute-done.5.far_low, f32[1024,128]{1,0:T(8,128)S(1)} %get-tuple-element.53.user_rated, ...), custom_call_target="tpu_custom_call" | custom-call | flops 270000000 | bytes 4000000 | tf_op jit(solution)/shard_map/pallas_call | solution.py:51
  43.4 2.6 %collective-permute-done.10.across_part = f32[128,128]{1,0:T(8,128)S(1)} collective-permute-done((f32[128,128]{1,0:T(8,128)S(1)}, f32[128,128]{1,0:T(8,128)S(1)}, u32[]{:S(2)}, u32[]{:S(2)}) %collective-permute-start.10) | collective-permute-done | bytes 65568 | tf_op jit(solution)/shard_map/ppermute | solution.py:341
  46.0 0.8 %shard_map.210 = (f32[128,128]{1,0:T(8,128)}, f32[1,128]{1,0:T(1,128)}) custom-call(f32[128,128]{1,0:T(8,128)S(1)} %get-tuple-element.62.mine, f32[128,128]{1,0:T(8,128)S(1)} %collective-permute-done.8.core_part, f32[128,128]{1,0:T(8,128)S(1)} %collective-permute-done.9.chip_part, f32[128,128]{1,0:T(8,128)S(1)} %collective-permute-done.10.across_part, ...), custom_call_target="tpu_custom_call" | custom-call | flops 1000000 | bytes 400000 | tf_op jit(solution)/shard_map/pallas_call | solution.py:51
  46.9 1.2 %shard_map.208 = (f32[1024,128]{1,0:T(8,128)}, f32[8,128]{1,0:T(8,128)}) custom-call(bf16[128,512]{1,0:T(8,128)(2,1)S(1)} %collective-permute-done.6.first, bf16[128,512]{1,0:T(8,128)(2,1)S(1)} %collective-permute-done.7.second, f32[1024,128]{1,0:T(8,128)S(1)} %copy-done.1, f32[8,128]{1,0:T(8,128)S(1)} %bitcast.10), custom_call_target="tpu_custom_call" | custom-call | flops 4000000 | bytes 1500000 | tf_op jit(solution)/shard_map/pallas_call | solution.py:51
  (20 shorter events, 0.7 us)
Async XLA Ops:
  3.2 30.2 %collective-permute-start.5 = (bf16[1024,128]{1,0:T(8,128)(2,1)S(1)}, bf16[1024,128]{1,0:T(8,128)(2,1)S(1)}, u32[]{:S(2)}, u32[]{:S(2)}) collective-permute-start(bf16[1024,128]{1,0:T(8,128)(2,1)S(1)} %get-tuple-element.48), channel_id=1, source_target_pairs={{0,128},{1,129},{2,130},{3,131},{4,132},{5,133},{6,134},{7,135},{8... | collective-permute-start | bytes 786440 | tf_op jit(solution)/shard_map/ppermute | solution.py:341
  7.0 20.0 %collective-permute-start.3 = (f32[264,128]{1,0:T(8,128)S(1)}, f32[264,128]{1,0:T(8,128)S(1)}, u32[]{:S(2)}, u32[]{:S(2)}) collective-permute-start(f32[264,128]{1,0:T(8,128)S(1)} %get-tuple-element.43), channel_id=1, source_target_pairs={{0,4},{1,5},{2,6},{3,7},{4,8},{5,9},{6,10},{7,11},{8,12},{9,13},{1... | collective-permute-start | bytes 405512 | tf_op jit(solution)/shard_map/ppermute | solution.py:341
  8.2 2.1 %collective-permute-start = (bf16[128,256]{1,0:T(8,128)(2,1)S(1)}, bf16[128,256]{1,0:T(8,128)(2,1)S(1)}, u32[]{:S(2)}, u32[]{:S(2)}) collective-permute-start(bf16[128,256]{1,0:T(8,128)(2,1)S(1)} %get-tuple-element.42), channel_id=1, source_target_pairs={{0,1},{1,0},{2,3},{3,2},{4,5},{5,4},{6,7},{7,6},{8,9},{9,8},{10,11... | collective-permute-start | bytes 196616 | tf_op jit(solution)/shard_map/ppermute | solution.py:341
  10.4 14.1 %collective-permute-start.2 = (bf16[128,256]{1,0:T(8,128)(2,1)S(1)}, bf16[128,256]{1,0:T(8,128)(2,1)S(1)}, u32[]{:S(2)}, u32[]{:S(2)}) collective-permute-start(bf16[128,256]{1,0:T(8,128)(2,1)S(1)} %shard_map.201), channel_id=1, source_target_pairs={{0,6},{1,7},{2,4},{3,5},{4,10},{5,11},{6,8},{7,9},{8,14},{9,15},{1... | collective-permute-start | bytes 196616 | tf_op jit(solution)/shard_map/ppermute | solution.py:341
  13.0 14.0 %collective-permute-start.1 = (bf16[128,256]{1,0:T(8,128)(2,1)S(1)}, bf16[128,256]{1,0:T(8,128)(2,1)S(1)}, u32[]{:S(2)}, u32[]{:S(2)}) collective-permute-start(bf16[128,256]{1,0:T(8,128)(2,1)S(1)} %shard_map.201), channel_id=1, source_target_pairs={{0,4},{1,5},{2,6},{3,7},{4,8},{5,9},{6,10},{7,11},{8,12},{9,13},{1... | collective-permute-start | bytes 196616 | tf_op jit(solution)/shard_map/ppermute | solution.py:341
  27.2 6.1 %collective-permute-start.4 = (bf16[256,128]{1,0:T(8,128)(2,1)S(1)}, bf16[256,128]{1,0:T(8,128)(2,1)S(1)}, u32[]{:S(2)}, u32[]{:S(2)}) collective-permute-start(bf16[256,128]{1,0:T(8,128)(2,1)S(1)} %get-tuple-element.44.own_low), channel_id=1, source_target_pairs={{0,1},{1,0},{2,3},{3,2},{4,5},{5,4},{6,7},{7,6},{8,9},{9,8},{10,11... | collective-permute-start | bytes 196616 | tf_op jit(solution)/shard_map/ppermute | solution.py:341
  28.6 3.8 %copy-start = (f32[1024,128]{1,0:T(8,128)S(1)}, f32[1024,128]{1,0:T(8,128)}, u32[]{:S(2)}) copy-start(f32[1024,128]{1,0:T(8,128)} %user.1) | copy-start | bytes 1572868
  28.7 3.8 %copy-start.2 = (f32[512,128]{1,0:T(8,128)S(1)}, f32[512,128]{1,0:T(8,128)}, u32[]{:S(2)}) copy-start(f32[512,128]{1,0:T(8,128)} %item.1) | copy-start | bytes 786436
  28.7 3.8 %copy-start.3 = (f32[1024]{0:T(1024)S(1)}, f32[1024]{0:T(1024)}, u32[]{:S(2)}) copy-start(f32[1024]{0:T(1024)} %param.17) | copy-start | bytes 12292
  35.8 11.0 %collective-permute-start.7 = (bf16[128,512]{1,0:T(8,128)(2,1)S(1)}, bf16[128,512]{1,0:T(8,128)(2,1)S(1)}, u32[]{:S(2)}, u32[]{:S(2)}) collective-permute-start(bf16[128,512]{1,0:T(8,128)(2,1)S(1)} %get-tuple-element.58), channel_id=1, source_target_pairs={{0,128},{1,129},{2,130},{3,131},{4,132},{5,133},{6,134},{7,135},{8... | collective-permute-start | bytes 393224 | tf_op jit(solution)/shard_map/ppermute | solution.py:341
  36.7 10.1 %collective-permute-start.6 = (bf16[128,512]{1,0:T(8,128)(2,1)S(1)}, bf16[128,512]{1,0:T(8,128)(2,1)S(1)}, u32[]{:S(2)}, u32[]{:S(2)}) collective-permute-start(bf16[128,512]{1,0:T(8,128)(2,1)S(1)} %get-tuple-element.57), channel_id=1, source_target_pairs={{0,128},{1,129},{2,130},{3,131},{4,132},{5,133},{6,134},{7,135},{8... | collective-permute-start | bytes 393224 | tf_op jit(solution)/shard_map/ppermute | solution.py:341
  38.9 8.0 %copy-start.1 = (f32[1024,128]{1,0:T(8,128)S(1)}, f32[1024,128]{1,0:T(8,128)}, u32[]{:S(2)}) copy-start(f32[1024,128]{1,0:T(8,128)} %friend.1) | copy-start | bytes 1572868
  38.9 8.0 %copy-start.4 = (f32[1024]{0:T(1024)S(1)}, f32[1024]{0:T(1024)}, u32[]{:S(2)}) copy-start(f32[1024]{0:T(1024)} %param.19) | copy-start | bytes 12292
  39.2 4.1 %collective-permute-start.8 = (f32[128,128]{1,0:T(8,128)S(1)}, f32[128,128]{1,0:T(8,128)S(1)}, u32[]{:S(2)}, u32[]{:S(2)}) collective-permute-start(f32[128,128]{1,0:T(8,128)S(1)} %get-tuple-element.63), channel_id=1, source_target_pairs={{0,1},{1,0},{2,3},{3,2},{4,5},{5,4},{6,7},{7,6},{8,9},{9,8},{10,11... | collective-permute-start | bytes 196616 | tf_op jit(solution)/shard_map/ppermute | solution.py:341
  39.8 3.6 %collective-permute-start.9 = (f32[128,128]{1,0:T(8,128)S(1)}, f32[128,128]{1,0:T(8,128)S(1)}, u32[]{:S(2)}, u32[]{:S(2)}) collective-permute-start(f32[128,128]{1,0:T(8,128)S(1)} %get-tuple-element.64), channel_id=1, source_target_pairs={{0,2},{1,3},{2,0},{3,1},{4,6},{5,7},{6,4},{7,5},{8,10},{9,11},{10,... | collective-permute-start | bytes 196616 | tf_op jit(solution)/shard_map/ppermute | solution.py:341
  41.3 4.7 %collective-permute-start.10 = (f32[128,128]{1,0:T(8,128)S(1)}, f32[128,128]{1,0:T(8,128)S(1)}, u32[]{:S(2)}, u32[]{:S(2)}) collective-permute-start(f32[128,128]{1,0:T(8,128)S(1)} %get-tuple-element.65), channel_id=1, source_target_pairs={{0,3},{1,2},{2,1},{3,0},{4,7},{5,6},{6,5},{7,4},{8,11},{9,10},{10,... | collective-permute-start | bytes 196616 | tf_op jit(solution)/shard_map/ppermute | solution.py:341

commit v2 on v1

--- a/solution.py
+++ b/solution.py
@@ -81,14 +81,11 @@
     return jnp.concatenate(halves, axis=0)
 
 
-def invert_slots(place_of, live, slots, places, spare):
-    @pl.loop(0, places)
-    def _(t):
+def invert_slots(place_of, live, slots, places, spare, total):
+    for t in range(places):
         slots[t] = spare
-
-    @pl.loop(0, live)
-    def _(q):
-        slots[place_of(q)] = q
+    for q in range(total):
+        slots[jnp.where(q < live, place_of(q), places)] = q
 
 
 def column_of(core, j):
@@ -100,43 +97,33 @@
 
 
 def first_stratum(
-    rows_hbm, cols_hbm, counts_hbm, user_hbm, item_hbm, acc_hbm, friend_hbm, vals_hbm, masks_hbm,
-    own_sum, other_sum, own_resid, other_resid, item_out, friend_low,
-    rows, cols, counts, user, item, acc, friend, vals, words, slots, right, sems,
+    rows_hbm, cols_hbm, counts_hbm, user_hbm, item_hbm, vals_hbm, masks_hbm,
+    own_sum, other_sum, own_resid, other_resid,
+    rows, cols, counts, user, item, vals, words, slots, right, sems,
 ):
     slot_total = vals_hbm.shape[1]
     core = lax.axis_index("grp") % 2
     sources = [
-        (vals_hbm.at[0], vals.at[pl.ds(0, slot_total)]),
-        (masks_hbm.at[0], words.at[:, pl.ds(0, slot_total), :]),
-        (user_hbm, user),
-        (item_hbm, item),
-        (acc_hbm, acc),
-        (friend_hbm, friend),
         (rows_hbm, rows),
         (cols_hbm, cols),
         (counts_hbm, counts),
+        (vals_hbm.at[0], vals.at[pl.ds(0, slot_total)]),
+        (masks_hbm.at[0], words.at[:, pl.ds(0, slot_total), :]),
+        (item_hbm, item),
+        (user_hbm, user),
     ]
     copies = [pltpu.make_async_copy(a, b, sems.at[i]) for i, (a, b) in enumerate(sources)]
-    for i in (6, 7, 8, 0, 1, 3, 4, 2, 5):
-        copies[i].start()
-    for i in (6, 7, 8):
-        copies[i].wait()
-    invert_slots(lambda q: rows[0, q] * 4 + cols[0, q], counts[0], slots, 32, slot_total)
+    for copy in copies:
+        copy.start()
+    for copy in copies[:3]:
+        copy.wait()
+    invert_slots(lambda q: rows[0, q] * 4 + cols[0, q], counts[0], slots, 32, slot_total, slot_total)
     zero_spare(words, slot_total)
     patterns = bit_patterns()
-    copies[3].wait()
+    copies[5].wait()
     for j in range(4):
-        column = column_of(core, j)
-        rows_f32 = item[pl.ds(pl.multiple_of(column * T, T), T), :]
-        right[tile(j), :] = rows_f32.astype(bf16)
-        if j < 2:
-            item_out[tile(j), :] = rows_f32
-    copies[4].wait()
-    item_out[2 * T : 2 * T + 8, :] = jnp.zeros((8, T), f32)
-    for j in range(2):
-        item_out[2 * T + j : 2 * T + j + 1, :] = acc[pl.ds(column_of(core, j), 1), :]
-    for i in (2, 1, 0):
+        right[tile(j), :] = item[pl.ds(pl.multiple_of(column_of(core, j) * T, T), T), :].astype(bf16)
+    for i in (6, 4, 3):
         copies[i].wait()
     user_low = user[...].astype(bf16)
     for r in range(8):
@@ -150,13 +137,17 @@
                 diff = vals[slot, part, :].astype(f32) - predict[part, tile(j)]
                 out[r * T + 16 * k2 : r * T + 16 * k2 + 16, tile(j % 2)] = jnp.where(seen, diff, 0.0).astype(bf16)
     own_sum[...] = matmul(user_low, own_resid[...], 0, 0)
-    other_sum[...] = matmul(user_low, other_resid[...], 0, 0).astype(bf16)
-    copies[5].wait()
+    other_sum[...] = matmul(user_low, other_resid[...], 0, 0)
+
+
+def chip_sum(own_sum, arrived, kept, sent):
+    total = own_sum[...] + arrived[...]
+    kept[...] = total
+    sent[...] = total.astype(bf16)
+
+
+def cast_friends(friend, friend_low):
     friend_low[...] = friend[...].astype(bf16)
-
-
-def chip_sum(own_sum, arrived, out):
-    out[...] = (own_sum[...] + arrived[...].astype(f32)).astype(bf16)
 
 
 def eye_mask():
@@ -213,7 +204,7 @@
     zero_spare(words, rate_total)
     zero_spare(trust_words, trust_total)
     patterns = bit_patterns()
-    invert_slots(lambda q: rows[1, q] * 4 + cols[1, q], counts[1], slots, 32, rate_total)
+    invert_slots(lambda q: rows[1, q] * 4 + cols[1, q], counts[1], slots, 32, rate_total, rate_total)
     copies[0].wait()
     copies[1].wait()
 
@@ -228,7 +219,7 @@
         for j in range(4):
             place(slots[r * 4 + column_of(core, j)], vals, words, placed, r, j)
 
-    invert_slots(lambda q: trust_rows[q] * 8 + trust_cols[q], trust_count[0], slots, 64, trust_total)
+    invert_slots(lambda q: trust_rows[q] * 8 + trust_cols[q], trust_count[0], slots, 64, trust_total, trust_total)
     copies[2].wait()
     copies[3].wait()
 
@@ -238,15 +229,22 @@
             place(slots[r * 8 + c], trust_vals, trust_words, trust_placed, r, c)
 
 
-def items_arrive(first, second, item_prev, item_mid, acc_mid, item_low):
+def update_items(kept, arrived, item, acc, share, item_low):
+    core = lax.axis_index("grp") % 2
+    near = lax.axis_index("grp") // 2
     eye = eye_mask()
-    total = first[...].astype(f32) + second[...].astype(f32)
+    total = kept[...] + arrived[...].astype(f32)
+    share[T : T + 8, :] = jnp.zeros((8, T), f32)
     for j in range(2):
-        acc_row = item_prev[2 * T + j : 2 * T + j + 1, :]
-        new, acc_out = update_rows(eye, item_prev[tile(j), :], acc_row, total[:, tile(j)].T)
-        item_mid[tile(j), :] = new
+        column = column_of(core, j)
+        factor = item[pl.ds(pl.multiple_of(column * T, T), T), :]
+        new, acc_out = update_rows(eye, factor, acc[pl.ds(column, 1), :], total[:, tile(j)].T)
         item_low[tile(j), :] = new.astype(bf16)
-        acc_mid[j : j + 1, :] = acc_out
+
+        @pl.when(near == j)
+        def _():
+            share[:T, :] = new
+            share[T : T + 1, :] = acc_out
 
 
 def residuals(left, right, placed, column, out):
@@ -259,8 +257,9 @@
             out[tile(r), tile(j)] = diff.astype(bf16)
 
 
-def own_columns(user_low, own_low, placed, own_resid):
+def own_columns(user_low, own_low, placed, own_resid, own_sum):
     residuals(user_low, own_low, placed, 0, own_resid)
+    own_sum[...] = matmul(user_low[...], own_resid[...], 0, 0)
 
 
 def second_stratum(
@@ -284,15 +283,15 @@
     friend_sum[...] = matmul(rated_low[...], trust_resid[...], 0, 0).astype(bf16)
 
 
-def item_products(user_low, own_resid, other_resid, mine, core_part, chip_part, across_part):
-    near = lax.axis_index("grp") // 2
-    own = matmul(user_low[...], own_resid[...], 0, 0)
-    other = matmul(user_low[...], other_resid[...], 0, 0)
-    flip = near == 1
-    mine[...] = jnp.where(flip, own[:, T:], own[:, :T])
-    chip_part[...] = jnp.where(flip, own[:, :T], own[:, T:])
-    core_part[...] = jnp.where(flip, other[:, T:], other[:, :T])
-    across_part[...] = jnp.where(flip, other[:, :T], other[:, T:])
+def item_products(user_low, other_resid, other_sum):
+    other_sum[...] = matmul(user_low[...], other_resid[...], 0, 0)
+
+
+def split_sum(own_sum, arrived, kept, sent):
+    flip = lax.axis_index("grp") // 2 == 1
+    total = own_sum[...] + arrived[...]
+    kept[...] = jnp.where(flip, total[:, T:], total[:, :T])
+    sent[...] = jnp.where(flip, total[:, :T], total[:, T:])
 
 
 def last_users(first_resid, second_resid, far_low, user_rated, acc_rated, user_out, acc_out):
@@ -305,11 +304,8 @@
         acc_out[r : r + 1, :] = acc
 
 
-def last_items(mine, core_part, chip_part, across_part, item_mid, acc_mid, item_out, acc_out):
-    near = lax.axis_index("grp") // 2
-    total = mine[...] + core_part[...] + chip_part[...] + across_part[...]
-    factor = item_mid[pl.ds(pl.multiple_of(near * T, T), T), :]
-    new, acc = update_rows(eye_mask(), factor, acc_mid[pl.ds(near, 1), :], total.T)
+def last_items(kept, arrived, share, item_out, acc_out):
+    new, acc = update_rows(eye_mask(), share[:T, :], share[T : T + 1, :], (kept[...] + arrived[...]).T)
     item_out[...] = new
     acc_out[...] = acc
 
@@ -347,30 +343,35 @@
     item_acc = item_accum.reshape(4, T)
     counts = rating_counts.reshape(2)
 
-    own_sum, other_sum, own_resid, other_resid, item_send, friend_low = call(
+    own_sum, other_sum, own_resid, other_resid = call(
         first_stratum,
-        [HBM] * 9,
-        [
-            shape((T, 2 * T), f32), shape((T, 2 * T), bf16), shape((8 * T, 2 * T), bf16), shape((8 * T, 2 * T), bf16),
-            shape((2 * T + 8, T), f32), shape((8 * T, T), bf16),
-        ],
+        [HBM] * 7,
+        [shape((T, 2 * T), f32), shape((T, 2 * T), f32), shape((8 * T, 2 * T), bf16), shape((8 * T, 2 * T), bf16)],
         [
             pltpu.SMEM((2, 32), jnp.int32), pltpu.SMEM((2, 32), jnp.int32), pltpu.SMEM((2,), jnp.int32),
-            pltpu.VMEM((8 * T, T), f32), pltpu.VMEM((4 * T, T), f32), pltpu.VMEM((4, T), f32), pltpu.VMEM((8 * T, T), f32),
-            pltpu.VMEM((33, T, T), bf16), pltpu.VMEM((10, 40, T), jnp.int32), pltpu.SMEM((32,), jnp.int32),
-            pltpu.VMEM((4 * T, T), bf16), pltpu.SemaphoreType.DMA((9,)),
+            pltpu.VMEM((8 * T, T), f32), pltpu.VMEM((4 * T, T), f32),
+            pltpu.VMEM((33, T, T), bf16), pltpu.VMEM((10, 40, T), jnp.int32), pltpu.SMEM((40,), jnp.int32),
+            pltpu.VMEM((4 * T, T), bf16), pltpu.SemaphoreType.DMA((7,)),
         ],
         270_000_000, 3_000_000,
-    )(rating_rows, rating_cols, counts, user_factors, item_factors, item_acc, friend_factors, rating_values, words_of)
-
-    other_arrived = send(other_sum, lambda b, g: (b, g ^ 1))
-    item_prev = send(item_send, lambda b, g: (b + 1, g))
-    chip = call(chip_sum, [VM, VM], [shape((T, 2 * T), bf16)], [], 100_000, 300_000)(own_sum, other_arrived)[0]
-    near_sum = send(chip, lambda b, g: (b + 1, g))
-    cross_sum = send(chip, lambda b, g: (b + 1, g ^ 2))
+    )(rating_rows, rating_cols, counts, user_factors, item_factors, rating_values, words_of)
+
+    arrived = send(other_sum, lambda b, g: (b, g ^ 1))
     half_bit = blocks // 2
+    friend_low = call(cast_friends, [VM], [shape((8 * T, T), bf16)], [], 100_000, 800_000)(friend_factors)[0]
     far_low = send(friend_low, lambda b, g: (b ^ half_bit, g))
-
+    kept, sent = call(
+        chip_sum, [VM, VM], [shape((T, 2 * T), f32), shape((T, 2 * T), bf16)], [], 100_000, 300_000
+    )(own_sum, arrived)
+    arrived = send(sent, lambda b, g: (b, g ^ 2))
+    share, own_low = call(
+        update_items,
+        [VM] * 4,
+        [shape((T + 8, T), f32), shape((2 * T, T), bf16)],
+        [], 1_000_000, 500_000,
+    )(kept, arrived, item_factors, item_acc)
+    own_low = send(own_low, lambda b, g: (b + 1, g))
+    share = send(share, lambda b, g: (b + 1, g))
     user_mid, acc_mid, user_low = call(
         first_users,
         [VM] * 5,
@@ -386,21 +387,18 @@
             pltpu.SMEM((48,), jnp.int32), pltpu.SMEM((48,), jnp.int32),
             pltpu.VMEM((33, T, T), bf16), pltpu.VMEM((10, 40, T), jnp.int32),
             pltpu.VMEM((49, T, T), bf16), pltpu.VMEM((10, 56, T), jnp.int32),
-            pltpu.SMEM((64,), jnp.int32), pltpu.SemaphoreType.DMA((9,)),
+            pltpu.SMEM((72,), jnp.int32), pltpu.SemaphoreType.DMA((9,)),
         ],
         20_000_000, 6_000_000,
     )(rating_rows, rating_cols, counts, trust_rows, trust_cols, trust_counts, rating_values, words_of, trust_values, trust_words_of)
 
-    item_mid, item_acc_mid, own_low = call(
-        items_arrive,
+    other_low = send(own_low, lambda b, g: (b, g ^ 1))
+    own_resid, own_sum = call(
+        own_columns,
         [VM] * 3,
-        [shape((2 * T, T), f32), shape((2, T), f32), shape((2 * T, T), bf16)],
-        [], 1_000_000, 500_000,
-    )(near_sum, cross_sum, item_prev)
-    other_low = send(own_low, lambda b, g: (b, g ^ 1))
-    own_resid = call(
-        own_columns, [VM] * 3, [shape((8 * T, 2 * T), bf16)], [], 67_000_000, 1_000_000
-    )(user_low, own_low, placed)[0]
+        [shape((8 * T, 2 * T), bf16), shape((T, 2 * T), f32)],
+        [], 140_000_000, 1_000_000,
+    )(user_low, own_low, placed)
     other_resid, user_rated, acc_rated, rated_low, trust_a, friend_a = call(
         second_stratum,
         [VM] * 9,
@@ -418,29 +416,23 @@
         [], 270_000_000, 3_000_000,
     )(rated_low, far_low, trust_placed)
     home_b = send(friend_b, lambda b, g: (b ^ half_bit, g))
-    mine, core_part, chip_part, across_part = call(
-        item_products,
-        [VM] * 3,
-        [shape((T, T), f32)] * 4,
-        [], 140_000_000, 1_500_000,
-    )(user_low, own_resid, other_resid)
-    core_part = send(core_part, lambda b, g: (b, g ^ 1))
-    chip_part = send(chip_part, lambda b, g: (b, g ^ 2))
-    across_part = send(across_part, lambda b, g: (b, g ^ 3))
+    other_sum = call(
+        item_products, [VM] * 2, [shape((T, 2 * T), f32)], [], 70_000_000, 900_000
+    )(user_low, other_resid)[0]
+    arrived = send(other_sum, lambda b, g: (b, g ^ 1))
     user_out, user_acc_out = call(
         last_users,
         [VM] * 5,
         [shape((8 * T, T), f32), shape((8, T), f32)],
         [], 270_000_000, 4_000_000,
     )(trust_a, trust_b, far_low, user_rated, acc_rated)
+    kept, sent = call(split_sum, [VM, VM], [shape((T, T), f32)] * 2, [], 100_000, 400_000)(own_sum, arrived)
+    arrived = send(sent, lambda b, g: (b, g ^ 2))
     item_out, item_acc_out = call(
-        last_items, [VM] * 6, [shape((T, T), f32), shape((1, T), f32)], [], 1_000_000, 400_000
-    )(mine, core_part, chip_part, across_part, item_mid, item_acc_mid)
+        last_items, [VM] * 3, [shape((T, T), f32), shape((1, T), f32)], [], 1_000_000, 400_000
+    )(kept, arrived, share)
     friend_out, friend_acc_out = call(
-        last_friends,
-        [VM] * 4,
-        [shape((8 * T, T), f32), shape((8, T), f32)],
-        [], 4_000_000, 1_500_000,
+        last_friends, [VM] * 4, [shape((8 * T, T), f32), shape((8, T), f32)], [], 4_000_000, 1_500_000
     )(home_a, home_b, friend_factors, friend_acc)
     return (
         user_out,

time: 48.1 us -> 46.9 us (0.975); the launches traced: 48 us -> 46.1 us
  starting transfers between devices: 16.1 us -> 14.7 us
    ppermute x11 -> x10, starting transfers between devices: 16.1 us -> 14.7 us  [send(): return lax.ppermute(value, axes, route)]
    pallas_call x12 -> x14, Pallas kernels: 13.7 us -> 13.4 us  [run(): return inner(*args)]
    ppermute x11 -> x10, waiting for transfers between devices: 16.8 us -> 16.5 us  [send(): return lax.ppermute(value, axes, route)]
  transfers between devices with their start and end apart: 11 -> 10, of which waited for: 5 -> 5; matrix products, arithmetic and copies ran while one was open for 0% -> 0% of each run, Pallas kernels for 16% -> 18%
where the time goes in v2:
time: 46.9 us; the launch traced here: 46.1 us
  waiting for transfers between devices  16.5 us (35%)
  starting transfers between devices  14.7 us (31%)
  Pallas kernels  13.4 us (29%)
  between operations  1.45 us (3%)
    ppermute x10, waiting for transfers between devices, send(): return lax.ppermute(value, axes, route)  16.5 us
    ppermute x10, starting transfers between devices, send(): return lax.ppermute(value, axes, route)  14.7 us
    pallas_call x14, Pallas kernels, run(): return inner(*args)  13.4 us
  transfers between devices with their start and end apart: 10, of which 5 were waited for; matrix products, arithmetic and copies ran while one was open for 0% of the time, Pallas kernels for 18%

profile of v2, /device:TPU:1, one launch (start us, length us, event | category | flops | bytes accessed | tf_op | source)
XLA Modules:
  0.0 46.1 jit_solution(5701416854619363091)
XLA Ops:
  0.7 2.5 %shard_map.199 = (f32[128,256]{1,0:T(8,128)S(1)}, f32[128,256]{1,0:T(8,128)S(1)}, bf16[1024,256]{1,0:T(8,128)(2,1)S(1)}, bf16[1024,256]{1,0:T(8,128)(2,1)S(1)}) custom-call(s32[2,32]{1,0:T(2,128)} %rows_hbm.3, s32[2,32]{1,0:T(2,128)} %cols_hbm.3, s32[2]{0:T(128)} %bitcast.15, f32[1024,128]{1,0:T(8,128)} %user.1, f32[512,128]{1,0:T(8,128)} %item.3, ...), custom_call_target="tpu_custom_call" | custom-call | flops 270000000 | bytes 3000000 | tf_op jit(solution)/shard_map/pallas_call | solution.py:51
  3.1 3.3 %collective-permute-start = (f32[128,256]{1,0:T(8,128)S(1)}, f32[128,256]{1,0:T(8,128)S(1)}, u32[]{:S(2)}, u32[]{:S(2)}) collective-permute-start(f32[128,256]{1,0:T(8,128)S(1)} %get-tuple-element.41), channel_id=1, source_target_pairs={{0,1},{1,0},{2,3},{3,2},{4,5},{5,4},{6,7},{7,6},{8,9},{9,8},{10,11... | collective-permute-start | bytes 393224 | tf_op jit(solution)/shard_map/ppermute | solution.py:337
  6.5 1.3 %collective-permute-start.4 = (bf16[1024,128]{1,0:T(8,128)(2,1)S(1)}, bf16[1024,128]{1,0:T(8,128)(2,1)S(1)}, u32[]{:S(2)}, u32[]{:S(2)}) collective-permute-start(bf16[1024,128]{1,0:T(8,128)(2,1)S(1)} %shard_map.205), channel_id=1, source_target_pairs={{0,128},{1,129},{2,130},{3,131},{4,132},{5,133},{6,134},{7,135},{8... | collective-permute-start | bytes 786440 | tf_op jit(solution)/shard_map/ppermute | solution.py:337
  7.8 1.7 %collective-permute-start.1 = (bf16[128,256]{1,0:T(8,128)(2,1)S(1)}, bf16[128,256]{1,0:T(8,128)(2,1)S(1)}, u32[]{:S(2)}, u32[]{:S(2)}) collective-permute-start(bf16[128,256]{1,0:T(8,128)(2,1)S(1)} %get-tuple-element.43), channel_id=1, source_target_pairs={{0,2},{1,3},{2,0},{3,1},{4,6},{5,7},{6,4},{7,5},{8,10},{9,11},{10,... | collective-permute-start | bytes 196616 | tf_op jit(solution)/shard_map/ppermute | solution.py:337
  9.5 2.1 %collective-permute-done.1.arrived = bf16[128,256]{1,0:T(8,128)(2,1)S(1)} collective-permute-done((bf16[128,256]{1,0:T(8,128)(2,1)S(1)}, bf16[128,256]{1,0:T(8,128)(2,1)S(1)}, u32[]{:S(2)}, u32[]{:S(2)}) %collective-permute-start.1) | collective-permute-done | bytes 65568 | tf_op jit(solution)/shard_map/ppermute | solution.py:337
  11.6 0.4 shard_map.202
  12.0 1.3 %collective-permute-start.2 = (bf16[256,128]{1,0:T(8,128)(2,1)S(1)}, bf16[256,128]{1,0:T(8,128)(2,1)S(1)}, u32[]{:S(2)}, u32[]{:S(2)}) collective-permute-start(bf16[256,128]{1,0:T(8,128)(2,1)S(1)} %get-tuple-element.44), channel_id=1, source_target_pairs={{0,4},{1,5},{2,6},{3,7},{4,8},{5,9},{6,10},{7,11},{8,12},{9,13},{1... | collective-permute-start | bytes 196616 | tf_op jit(solution)/shard_map/ppermute | solution.py:337
  13.3 8.7 %collective-permute-done.2.own_low = bf16[256,128]{1,0:T(8,128)(2,1)S(1)} collective-permute-done((bf16[256,128]{1,0:T(8,128)(2,1)S(1)}, bf16[256,128]{1,0:T(8,128)(2,1)S(1)}, u32[]{:S(2)}, u32[]{:S(2)}) %collective-permute-start.2) | collective-permute-done | bytes 65568 | tf_op jit(solution)/shard_map/ppermute | solution.py:337
  21.9 2.7 %collective-permute-start.3 = (bf16[256,128]{1,0:T(8,128)(2,1)S(1)}, bf16[256,128]{1,0:T(8,128)(2,1)S(1)}, u32[]{:S(2)}, u32[]{:S(2)}) collective-permute-start(bf16[256,128]{1,0:T(8,128)(2,1)S(1)} %collective-permute-done.2.own_low), channel_id=1, source_target_pairs={{0,1},{1,0},{2,3},{3,2},{4,5},{5,4},{6,7},{7,6},{8,9},{9,8},{10,11... | collective-permute-start | bytes 196616 | tf_op jit(solution)/shard_map/ppermute | solution.py:337
  25.3 3.0 %shard_map.203 = (bf16[1024,512]{1,0:T(8,128)(2,1)S(1)}, bf16[1024,1024]{1,0:T(8,128)(2,1)S(1)}) custom-call(s32[2,32]{1,0:T(2,128)} %rows_hbm.3, s32[2,32]{1,0:T(2,128)} %cols_hbm.3, s32[2]{0:T(128)} %bitcast.16, s32[48]{0:T(128)} %trust_rows_hbm.1, s32[48]{0:T(128)} %trust_cols_hbm.1, s32[1]{0:T(128)S(6)} %copy.22.trust_count, ...), custom_call_target="tpu_custom_call" | custom-call | flops 20000000 | bytes 6000000 | tf_op jit(solution)/shard_map/pallas_call | solution.py:51
  28.4 0.5 %shard_map.200 = (f32[1024,128]{1,0:T(8,128)S(1)}, f32[8,128]{1,0:T(8,128)S(1)}, bf16[1024,128]{1,0:T(8,128)(2,1)S(1)}) custom-call(bf16[1024,256]{1,0:T(8,128)(2,1)S(1)} %get-tuple-element.37.own_resid, bf16[1024,256]{1,0:T(8,128)(2,1)S(1)} %get-tuple-element.38.other_resid, f32[1024,128]{1,0:T(8,128)S(1)} %copy-done.2, f32[512,128]{1,0:T(8,128)S(1)} %copy-done, ...), custom_call_target="tpu_custom_call" | custom-call | flops 140000000 | bytes 3000000 | tf_op jit(solution)/shard_map/pallas_call | solution.py:51
  28.9 0.6 %shard_map.204 = (bf16[1024,256]{1,0:T(8,128)(2,1)S(1)}, f32[128,256]{1,0:T(8,128)S(1)}) custom-call(bf16[1024,128]{1,0:T(8,128)(2,1)S(1)} %get-tuple-element.39.user_low, bf16[256,128]{1,0:T(8,128)(2,1)S(1)} %collective-permute-done.2.own_low, bf16[1024,512]{1,0:T(8,128)(2,1)S(1)} %get-tuple-element.45.placed), custom_call_target="tpu_custom_call" | custom-call | flops 140000000 | bytes 1000000 | tf_op jit(solution)/shard_map/pallas_call | solution.py:51
  29.5 1.7 %shard_map.206 = (bf16[1024,256]{1,0:T(8,128)(2,1)S(1)}, f32[1024,128]{1,0:T(8,128)S(1)}, f32[8,128]{1,0:T(8,128)S(1)}, bf16[1024,128]{1,0:T(8,128)(2,1)S(1)}, b...) custom-call(bf16[1024,128]{1,0:T(8,128)(2,1)S(1)} %get-tuple-element.39.user_low, ...), custom_call_target="tpu_custom_call" | custom-call | flops 400000000 | bytes 6000000 | tf_op jit(solution)/shard_map/pallas_call | solution.py:51
  31.2 0.3 shard_map.210
  31.6 0.7 %shard_map.207 = (bf16[1024,512]{1,0:T(8,128)(2,1)S(1)}, bf16[128,512]{1,0:T(8,128)(2,1)S(1)}) custom-call(bf16[1024,128]{1,0:T(8,128)(2,1)S(1)} %get-tuple-element.51.rated_low, bf16[1024,128]{1,0:T(8,128)(2,1)S(1)} %collective-permute-done.4.far_low, bf16[1024,1024]{1,0:T(8,128)(2,1)S(1)} %get-tuple-element.49.trust_placed), custom_call_target="tpu_custom_call" | custom-call | flops 270000000 | bytes 3000000 | tf_op jit(solution)/shard_map/pallas_call | solution.py:51
  32.4 1.6 %collective-permute-start.6 = (bf16[128,512]{1,0:T(8,128)(2,1)S(1)}, bf16[128,512]{1,0:T(8,128)(2,1)S(1)}, u32[]{:S(2)}, u32[]{:S(2)}) collective-permute-start(bf16[128,512]{1,0:T(8,128)(2,1)S(1)} %get-tuple-element.58), channel_id=1, source_target_pairs={{0,128},{1,129},{2,130},{3,131},{4,132},{5,133},{6,134},{7,135},{8... | collective-permute-start | bytes 393224 | tf_op jit(solution)/shard_map/ppermute | solution.py:337
  33.9 1.5 %collective-permute-start.5 = (bf16[128,512]{1,0:T(8,128)(2,1)S(1)}, bf16[128,512]{1,0:T(8,128)(2,1)S(1)}, u32[]{:S(2)}, u32[]{:S(2)}) collective-permute-start(bf16[128,512]{1,0:T(8,128)(2,1)S(1)} %get-tuple-element.57), channel_id=1, source_target_pairs={{0,128},{1,129},{2,130},{3,131},{4,132},{5,133},{6,134},{7,135},{8... | collective-permute-start | bytes 393224 | tf_op jit(solution)/shard_map/ppermute | solution.py:337
  35.5 1.3 %collective-permute-start.8 = (f32[128,128]{1,0:T(8,128)S(1)}, f32[128,128]{1,0:T(8,128)S(1)}, u32[]{:S(2)}, u32[]{:S(2)}) collective-permute-start(f32[128,128]{1,0:T(8,128)S(1)} %get-tuple-element.64), channel_id=1, source_target_pairs={{0,2},{1,3},{2,0},{3,1},{4,6},{5,7},{6,4},{7,5},{8,10},{9,11},{10,... | collective-permute-start | bytes 196616 | tf_op jit(solution)/shard_map/ppermute | solution.py:337
  36.8 1.6 %shard_map.208 = (f32[1024,128]{1,0:T(8,128)}, f32[8,128]{1,0:T(8,128)}) custom-call(bf16[1024,512]{1,0:T(8,128)(2,1)S(1)} %get-tuple-element.50.first_resid, bf16[1024,512]{1,0:T(8,128)(2,1)S(1)} %get-tuple-element.52.second_resid, bf16[1024,128]{1,0:T(8,128)(2,1)S(1)} %collective-permute-done.4.far_low, f32[1024,128]{1,0:T(8,128)S(1)} %get-tuple-element.53.user_rated, ...), custom_call_target="tpu_custom_call" | custom-call | flops 270000000 | bytes 4000000 | tf_op jit(solution)/shard_map/pallas_call | solution.py:51
  38.4 0.1 collective-permute-done.6.second
  38.5 2.8 %collective-permute-done.5.first = bf16[128,512]{1,0:T(8,128)(2,1)S(1)} collective-permute-done((bf16[128,512]{1,0:T(8,128)(2,1)S(1)}, bf16[128,512]{1,0:T(8,128)(2,1)S(1)}, u32[]{:S(2)}, u32[]{:S(2)}) %collective-permute-start.5) | collective-permute-done | bytes 131104 | tf_op jit(solution)/shard_map/ppermute | solution.py:337
  41.3 1.2 %shard_map.209 = (f32[1024,128]{1,0:T(8,128)}, f32[8,128]{1,0:T(8,128)}) custom-call(bf16[128,512]{1,0:T(8,128)(2,1)S(1)} %collective-permute-done.5.first, bf16[128,512]{1,0:T(8,128)(2,1)S(1)} %collective-permute-done.6.second, f32[1024,128]{1,0:T(8,128)S(1)} %copy-done.1, f32[8,128]{1,0:T(8,128)S(1)} %bitcast.10), custom_call_target="tpu_custom_call" | custom-call | flops 4000000 | bytes 1500000 | tf_op jit(solution)/shard_map/pallas_call | solution.py:51
  42.5 2.8 %collective-permute-done.9.share = f32[136,128]{1,0:T(8,128)S(1)} collective-permute-done((f32[136,128]{1,0:T(8,128)S(1)}, f32[136,128]{1,0:T(8,128)S(1)}, u32[]{:S(2)}, u32[]{:S(2)}) %collective-permute-start.9) | collective-permute-done | bytes 69664 | tf_op jit(solution)/shard_map/ppermute | solution.py:337
  45.3 0.8 %shard_map.212 = (f32[128,128]{1,0:T(8,128)}, f32[1,128]{1,0:T(1,128)}) custom-call(f32[128,128]{1,0:T(8,128)S(1)} %get-tuple-element.63.kept, f32[128,128]{1,0:T(8,128)S(1)} %collective-permute-done.8.arrived, f32[136,128]{1,0:T(8,128)S(1)} %collective-permute-done.9.share), custom_call_target="tpu_custom_call" | custom-call | flops 1000000 | bytes 400000 | tf_op jit(solution)/shard_map/pallas_call | solution.py:51
  (22 shorter events, 0.2 us)
Async XLA Ops:
  0.6 5.8 %copy-start.1 = (f32[1024,128]{1,0:T(8,128)S(1)}, f32[1024,128]{1,0:T(8,128)}, u32[]{:S(2)}) copy-start(f32[1024,128]{1,0:T(8,128)} %friend.3) | copy-start | bytes 1572868
  0.6 10.9 %copy-start = (f32[512,128]{1,0:T(8,128)S(1)}, f32[512,128]{1,0:T(8,128)}, u32[]{:S(2)}) copy-start(f32[512,128]{1,0:T(8,128)} %item.3) | copy-start | bytes 786436
  0.7 10.9 %copy-start.5 = (f32[512]{0:T(512)S(1)}, f32[512]{0:T(512)}, u32[]{:S(2)}) copy-start(f32[512]{0:T(512)} %param.21) | copy-start | bytes 6148
  3.1 4.6 %collective-permute-start = (f32[128,256]{1,0:T(8,128)S(1)}, f32[128,256]{1,0:T(8,128)S(1)}, u32[]{:S(2)}, u32[]{:S(2)}) collective-permute-start(f32[128,256]{1,0:T(8,128)S(1)} %get-tuple-element.41), channel_id=1, source_target_pairs={{0,1},{1,0},{2,3},{3,2},{4,5},{5,4},{6,7},{7,6},{8,9},{9,8},{10,11... | collective-permute-start | bytes 393224 | tf_op jit(solution)/shard_map/ppermute | solution.py:337
  6.5 23.0 %collective-permute-start.4 = (bf16[1024,128]{1,0:T(8,128)(2,1)S(1)}, bf16[1024,128]{1,0:T(8,128)(2,1)S(1)}, u32[]{:S(2)}, u32[]{:S(2)}) collective-permute-start(bf16[1024,128]{1,0:T(8,128)(2,1)S(1)} %shard_map.205), channel_id=1, source_target_pairs={{0,128},{1,129},{2,130},{3,131},{4,132},{5,133},{6,134},{7,135},{8... | collective-permute-start | bytes 786440 | tf_op jit(solution)/shard_map/ppermute | solution.py:337
  7.8 3.8 %collective-permute-start.1 = (bf16[128,256]{1,0:T(8,128)(2,1)S(1)}, bf16[128,256]{1,0:T(8,128)(2,1)S(1)}, u32[]{:S(2)}, u32[]{:S(2)}) collective-permute-start(bf16[128,256]{1,0:T(8,128)(2,1)S(1)} %get-tuple-element.43), channel_id=1, source_target_pairs={{0,2},{1,3},{2,0},{3,1},{4,6},{5,7},{6,4},{7,5},{8,10},{9,11},{10,... | collective-permute-start | bytes 196616 | tf_op jit(solution)/shard_map/ppermute | solution.py:337
  12.0 10.0 %collective-permute-start.2 = (bf16[256,128]{1,0:T(8,128)(2,1)S(1)}, bf16[256,128]{1,0:T(8,128)(2,1)S(1)}, u32[]{:S(2)}, u32[]{:S(2)}) collective-permute-start(bf16[256,128]{1,0:T(8,128)(2,1)S(1)} %get-tuple-element.44), channel_id=1, source_target_pairs={{0,4},{1,5},{2,6},{3,7},{4,8},{5,9},{6,10},{7,11},{8,12},{9,13},{1... | collective-permute-start | bytes 196616 | tf_op jit(solution)/shard_map/ppermute | solution.py:337
  21.9 7.6 %collective-permute-start.3 = (bf16[256,128]{1,0:T(8,128)(2,1)S(1)}, bf16[256,128]{1,0:T(8,128)(2,1)S(1)}, u32[]{:S(2)}, u32[]{:S(2)}) collective-permute-start(bf16[256,128]{1,0:T(8,128)(2,1)S(1)} %collective-permute-done.2.own_low), channel_id=1, source_target_pairs={{0,1},{1,0},{2,3},{3,2},{4,5},{5,4},{6,7},{7,6},{8,9},{9,8},{10,11... | collective-permute-start | bytes 196616 | tf_op jit(solution)/shard_map/ppermute | solution.py:337
  25.3 3.1 %copy-start.2 = (f32[1024,128]{1,0:T(8,128)S(1)}, f32[1024,128]{1,0:T(8,128)}, u32[]{:S(2)}) copy-start(f32[1024,128]{1,0:T(8,128)} %user.1) | copy-start | bytes 1572868
  25.3 3.1 %copy-start.3 = (f32[1024]{0:T(1024)S(1)}, f32[1024]{0:T(1024)}, u32[]{:S(2)}) copy-start(f32[1024]{0:T(1024)} %param.17) | copy-start | bytes 12292
  31.5 3.9 %collective-permute-start.7 = (f32[128,256]{1,0:T(8,128)S(1)}, f32[128,256]{1,0:T(8,128)S(1)}, u32[]{:S(2)}, u32[]{:S(2)}) collective-permute-start(f32[128,256]{1,0:T(8,128)S(1)} %shard_map.210), channel_id=1, source_target_pairs={{0,1},{1,0},{2,3},{3,2},{4,5},{5,4},{6,7},{7,6},{8,9},{9,8},{10,11... | collective-permute-start | bytes 393224 | tf_op jit(solution)/shard_map/ppermute | solution.py:337
  32.3 9.0 %copy-start.4 = (f32[1024]{0:T(1024)S(1)}, f32[1024]{0:T(1024)}, u32[]{:S(2)}) copy-start(f32[1024]{0:T(1024)} %param.19) | copy-start | bytes 12292
  32.4 6.2 %collective-permute-start.6 = (bf16[128,512]{1,0:T(8,128)(2,1)S(1)}, bf16[128,512]{1,0:T(8,128)(2,1)S(1)}, u32[]{:S(2)}, u32[]{:S(2)}) collective-permute-start(bf16[128,512]{1,0:T(8,128)(2,1)S(1)} %get-tuple-element.58), channel_id=1, source_target_pairs={{0,128},{1,129},{2,130},{3,131},{4,132},{5,133},{6,134},{7,135},{8... | collective-permute-start | bytes 393224 | tf_op jit(solution)/shard_map/ppermute | solution.py:337
  33.9 7.4 %collective-permute-start.5 = (bf16[128,512]{1,0:T(8,128)(2,1)S(1)}, bf16[128,512]{1,0:T(8,128)(2,1)S(1)}, u32[]{:S(2)}, u32[]{:S(2)}) collective-permute-start(bf16[128,512]{1,0:T(8,128)(2,1)S(1)} %get-tuple-element.57), channel_id=1, source_target_pairs={{0,128},{1,129},{2,130},{3,131},{4,132},{5,133},{6,134},{7,135},{8... | collective-permute-start | bytes 393224 | tf_op jit(solution)/shard_map/ppermute | solution.py:337
  35.4 9.9 %collective-permute-start.9 = (f32[136,128]{1,0:T(8,128)S(1)}, f32[136,128]{1,0:T(8,128)S(1)}, u32[]{:S(2)}, u32[]{:S(2)}) collective-permute-start(f32[136,128]{1,0:T(8,128)S(1)} %get-tuple-element.65), channel_id=1, source_target_pairs={{0,4},{1,5},{2,6},{3,7},{4,8},{5,9},{6,10},{7,11},{8,12},{9,13},{1... | collective-permute-start | bytes 208904 | tf_op jit(solution)/shard_map/ppermute | solution.py:337
  35.5 9.8 %collective-permute-start.8 = (f32[128,128]{1,0:T(8,128)S(1)}, f32[128,128]{1,0:T(8,128)S(1)}, u32[]{:S(2)}, u32[]{:S(2)}) collective-permute-start(f32[128,128]{1,0:T(8,128)S(1)} %get-tuple-element.64), channel_id=1, source_target_pairs={{0,2},{1,3},{2,0},{3,1},{4,6},{5,7},{6,4},{7,5},{8,10},{9,11},{10,... | collective-permute-start | bytes 196616 | tf_op jit(solution)/shard_map/ppermute | solution.py:337

commit v3 on v2

--- a/solution.py
+++ b/solution.py
@@ -32,13 +32,14 @@
     return slice(index * T, (index + 1) * T)
 
 
-def call(body, ins, outs, scratch, flops, moved):
+def call(body, ins, outs, scratch, flops, moved, out_specs=None, aliases=None):
     inner = pl.pallas_call(
         body,
         in_specs=ins,
-        out_specs=[VM] * len(outs),
+        out_specs=out_specs or [VM] * len(outs),
         out_shape=outs,
         scratch_shapes=scratch,
+        input_output_aliases=aliases or {},
         cost_estimate=pl.CostEstimate(flops=flops, bytes_accessed=moved, transcendentals=0),
         compiler_params=pltpu.CompilerParams(vmem_limit_bytes=GRANT),
     )
@@ -107,10 +108,10 @@
         (rows_hbm, rows),
         (cols_hbm, cols),
         (counts_hbm, counts),
-        (vals_hbm.at[0], vals.at[pl.ds(0, slot_total)]),
-        (masks_hbm.at[0], words.at[:, pl.ds(0, slot_total), :]),
         (item_hbm, item),
         (user_hbm, user),
+        (masks_hbm.at[0], words.at[:, pl.ds(0, slot_total), :]),
+        (vals_hbm.at[0], vals.at[pl.ds(0, slot_total)]),
     ]
     copies = [pltpu.make_async_copy(a, b, sems.at[i]) for i, (a, b) in enumerate(sources)]
     for copy in copies:
@@ -120,24 +121,27 @@
     invert_slots(lambda q: rows[0, q] * 4 + cols[0, q], counts[0], slots, 32, slot_total, slot_total)
     zero_spare(words, slot_total)
     patterns = bit_patterns()
-    copies[5].wait()
+    copies[3].wait()
     for j in range(4):
         right[tile(j), :] = item[pl.ds(pl.multiple_of(column_of(core, j) * T, T), T), :].astype(bf16)
-    for i in (6, 4, 3):
-        copies[i].wait()
+    copies[4].wait()
     user_low = user[...].astype(bf16)
+    predict = matmul(user_low[: 2 * T, :], right[...], 1, 1)
+    copies[5].wait()
+    copies[6].wait()
     for r in range(8):
-        predict = matmul(user_low[tile(r), :], right[...], 1, 1)
+        if r and r % 2 == 0:
+            predict = matmul(user_low[r * T : (r + 2) * T, :], right[...], 1, 1)
         for j in range(4):
             slot = slots[r * 4 + column_of(core, j)]
             out = own_resid if j < 2 else other_resid
             for k2 in range(T // 16):
                 part = slice(16 * k2, 16 * k2 + 16)
                 seen = observed(patterns, words, slot, k2)
-                diff = vals[slot, part, :].astype(f32) - predict[part, tile(j)]
-                out[r * T + 16 * k2 : r * T + 16 * k2 + 16, tile(j % 2)] = jnp.where(seen, diff, 0.0).astype(bf16)
-    own_sum[...] = matmul(user_low, own_resid[...], 0, 0)
-    other_sum[...] = matmul(user_low, other_resid[...], 0, 0)
+                diff = vals[slot, part, :].astype(f32) - predict[r % 2 * T + 16 * k2 : r % 2 * T + 16 * k2 + 16, tile(j)]
+                out[j % 2, r * T + 16 * k2 : r * T + 16 * k2 + 16, :] = jnp.where(seen, diff, 0.0).astype(bf16)
+    own_sum[...] = matmul(user_low, side(own_resid), 0, 0)
+    other_sum[...] = matmul(user_low, side(other_resid), 0, 0)
 
 
 def chip_sum(own_sum, arrived, kept, sent):
@@ -170,7 +174,7 @@
     for first in (0, 2):
         parts = [item[pl.ds(pl.multiple_of(column_of(core, j) * T, T), T), :] for j in (first, first + 1)]
         halves.append(jnp.concatenate(parts, axis=0).astype(bf16))
-    prod = matmul(own_resid[...], halves[0], 1, 0) + matmul(other_resid[...], halves[1], 1, 0)
+    prod = matmul(side(own_resid), halves[0], 1, 0) + matmul(side(other_resid), halves[1], 1, 0)
     for r in range(8):
         new, acc_out = update_rows(eye, user[tile(r), :], acc[r : r + 1, :], prod[tile(r), :])
         user_mid[tile(r), :] = new
@@ -212,7 +216,7 @@
         for k2 in range(T // 16):
             seen = observed(patterns, packed, slot, k2)
             value = jnp.where(seen, values[slot, 16 * k2 : 16 * k2 + 16, :].astype(f32), UNSEEN)
-            out[pl.ds(pl.multiple_of(r * T + 16 * k2, 16), 16), tile(c)] = value.astype(bf16)
+            out[c, pl.ds(pl.multiple_of(r * T + 16 * k2, 16), 16), :] = value
 
     @pl.loop(0, 8)
     def _(r):
@@ -247,44 +251,50 @@
             share[T : T + 1, :] = acc_out
 
 
-def residuals(left, right, placed, column, out):
+def side(resid):
+    return jnp.concatenate([resid[j] for j in range(resid.shape[0])], axis=1)
+
+
+def residuals(left, right, placed, column, out, height=8):
     count = right.shape[0] // T
-    for r in range(8):
-        predict = matmul(left[tile(r), :], right[...], 1, 1)
+    for r in range(8 // height):
+        part = slice(r * height * T, (r + 1) * height * T)
+        predict = matmul(left[part, :], right[...], 1, 1)
         for j in range(count):
-            value = placed[tile(r), tile(column + j)].astype(f32)
-            diff = jnp.where(value < SEEN_BELOW, value - predict[:, tile(j)], 0.0)
-            out[tile(r), tile(j)] = diff.astype(bf16)
-
-
-def own_columns(user_low, own_low, placed, own_resid, own_sum):
-    residuals(user_low, own_low, placed, 0, own_resid)
-    own_sum[...] = matmul(user_low[...], own_resid[...], 0, 0)
+            value = placed[column + j, part, :]
+            out[j, part, :] = jnp.where(value < SEEN_BELOW, value - predict[:, tile(j)], 0.0).astype(bf16)
+
+
+def own_columns(user_low, own_low, placed, own_resid, own_sum, own_prod):
+    residuals(user_low, own_low, placed, 0, own_resid, 2)
+    resid = side(own_resid)
+    own_sum[...] = matmul(user_low[...], resid, 0, 0)
+    own_prod[...] = matmul(resid, own_low[...], 1, 0)
 
 
 def second_stratum(
-    user_low, own_low, other_low, placed, own_resid, user_mid, acc_mid, far_low, trust_placed,
+    user_low, other_low, placed, own_prod, user_mid, acc_mid, far_low, trust_placed,
     other_resid, user_rated, acc_rated, rated_low, trust_resid, friend_sum,
 ):
     eye = eye_mask()
     residuals(user_low, other_low, placed, 2, other_resid)
-    prod = matmul(own_resid[...], own_low[...], 1, 0) + matmul(other_resid[...], other_low[...], 1, 0)
+    prod = own_prod[...] + matmul(side(other_resid), other_low[...], 1, 0)
     for r in range(8):
         new, acc_out = update_rows(eye, user_mid[tile(r), :], acc_mid[r : r + 1, :], prod[tile(r), :])
         user_rated[tile(r), :] = new
         rated_low[tile(r), :] = new.astype(bf16)
         acc_rated[r : r + 1, :] = acc_out
     residuals(rated_low, far_low.at[pl.ds(0, 4 * T)], trust_placed, 0, trust_resid)
-    friend_sum[...] = matmul(rated_low[...], trust_resid[...], 0, 0).astype(bf16)
+    friend_sum[...] = matmul(rated_low[...], side(trust_resid), 0, 0).astype(bf16)
 
 
 def second_half(rated_low, far_low, trust_placed, trust_resid, friend_sum):
     residuals(rated_low, far_low.at[pl.ds(4 * T, 4 * T)], trust_placed, 4, trust_resid)
-    friend_sum[...] = matmul(rated_low[...], trust_resid[...], 0, 0).astype(bf16)
+    friend_sum[...] = matmul(rated_low[...], side(trust_resid), 0, 0).astype(bf16)
 
 
 def item_products(user_low, other_resid, other_sum):
-    other_sum[...] = matmul(user_low[...], other_resid[...], 0, 0)
+    other_sum[...] = matmul(user_low[...], side(other_resid), 0, 0)
 
 
 def split_sum(own_sum, arrived, kept, sent):
@@ -297,27 +307,48 @@
 def last_users(first_resid, second_resid, far_low, user_rated, acc_rated, user_out, acc_out):
     eye = eye_mask()
     half = 4 * T
-    prod = matmul(first_resid[...], far_low[:half, :], 1, 0) + matmul(second_resid[...], far_low[half:, :], 1, 0)
+    prod = matmul(side(first_resid), far_low[:half, :], 1, 0) + matmul(side(second_resid), far_low[half:, :], 1, 0)
     for r in range(8):
         new, acc = update_rows(eye, user_rated[tile(r), :], acc_rated[r : r + 1, :], prod[tile(r), :])
         user_out[tile(r), :] = new
         acc_out[r : r + 1, :] = acc
 
 
-def last_items(kept, arrived, share, item_out, acc_out):
-    new, acc = update_rows(eye_mask(), share[:T, :], share[T : T + 1, :], (kept[...] + arrived[...]).T)
-    item_out[...] = new
-    acc_out[...] = acc
-
-
-def last_friends(first, second, friend, acc, friend_out, acc_out):
+def friend_rows(eye, home, friend, acc, first, rows, acc_rows):
+    for j in range(4):
+        r = first + j
+        new, acc_row = update_rows(eye, friend[tile(r), :], acc[r : r + 1, :], home[:, tile(j)].astype(f32).T)
+        rows[tile(j), :] = new
+        acc_rows[r : r + 1, :] = acc_row
+
+
+def move_out(pairs, sems):
+    copies = [pltpu.make_async_copy(a, b, sems.at[i]) for i, (a, b) in enumerate(pairs)]
+    for copy in copies:
+        copy.start()
+    for copy in copies:
+        copy.wait()
+
+
+def first_friends(
+    home, friend, acc, kept, arrived, share,
+    friend_out, item_out, item_acc_out, acc_rows,
+    rows, item_rows, item_acc, sems,
+):
     eye = eye_mask()
-    for r in range(8):
-        arrived = first if r < 4 else second
-        prod = arrived[:, tile(r % 4)].astype(f32).T
-        new, acc_row = update_rows(eye, friend[tile(r), :], acc[r : r + 1, :], prod)
-        friend_out[tile(r), :] = new
-        acc_out[r : r + 1, :] = acc_row
+    new, acc_row = update_rows(eye, share[:T, :], share[T : T + 1, :], (kept[...] + arrived[...]).T)
+    item_rows[...] = new
+    item_acc[...] = acc_row
+    acc_rows[4:8, :] = acc[4:8, :]
+    friend_rows(eye, home, friend, acc, 0, rows, acc_rows)
+    move_out([(rows, friend_out.at[pl.ds(0, 4 * T)]), (item_rows, item_out), (item_acc, item_acc_out)], sems)
+
+
+def other_friends(home, friend, acc, earlier, friend_out, acc_out, rows, acc_rows, sems):
+    del earlier
+    acc_rows[0:4, :] = acc[0:4, :]
+    friend_rows(eye_mask(), home, friend, acc, 4, rows, acc_rows)
+    move_out([(rows, friend_out.at[pl.ds(4 * T, 4 * T)]), (acc_rows, acc_out)], sems)
 
 
 def local(
@@ -346,7 +377,7 @@
     own_sum, other_sum, own_resid, other_resid = call(
         first_stratum,
         [HBM] * 7,
-        [shape((T, 2 * T), f32), shape((T, 2 * T), f32), shape((8 * T, 2 * T), bf16), shape((8 * T, 2 * T), bf16)],
+        [shape((T, 2 * T), f32), shape((T, 2 * T), f32), shape((2, 8 * T, T), bf16), shape((2, 8 * T, T), bf16)],
         [
             pltpu.SMEM((2, 32), jnp.int32), pltpu.SMEM((2, 32), jnp.int32), pltpu.SMEM((2,), jnp.int32),
             pltpu.VMEM((8 * T, T), f32), pltpu.VMEM((4 * T, T), f32),
@@ -381,7 +412,7 @@
     placed, trust_placed = call(
         place_tiles,
         [HBM] * 5 + [SM] + [HBM] * 4,
-        [shape((8 * T, 4 * T), bf16), shape((8 * T, 8 * T), bf16)],
+        [shape((4, 8 * T, T), f32), shape((8, 8 * T, T), f32)],
         [
             pltpu.SMEM((2, 32), jnp.int32), pltpu.SMEM((2, 32), jnp.int32), pltpu.SMEM((2,), jnp.int32),
             pltpu.SMEM((48,), jnp.int32), pltpu.SMEM((48,), jnp.int32),
@@ -393,26 +424,26 @@
     )(rating_rows, rating_cols, counts, trust_rows, trust_cols, trust_counts, rating_values, words_of, trust_values, trust_words_of)
 
     other_low = send(own_low, lambda b, g: (b, g ^ 1))
-    own_resid, own_sum = call(
+    _, own_sum, own_prod = call(
         own_columns,
         [VM] * 3,
-        [shape((8 * T, 2 * T), bf16), shape((T, 2 * T), f32)],
-        [], 140_000_000, 1_000_000,
+        [shape((2, 8 * T, T), bf16), shape((T, 2 * T), f32), shape((8 * T, T), f32)],
+        [], 200_000_000, 1_500_000,
     )(user_low, own_low, placed)
     other_resid, user_rated, acc_rated, rated_low, trust_a, friend_a = call(
         second_stratum,
-        [VM] * 9,
+        [VM] * 8,
         [
-            shape((8 * T, 2 * T), bf16), shape((8 * T, T), f32), shape((8, T), f32), shape((8 * T, T), bf16),
-            shape((8 * T, 4 * T), bf16), shape((T, 4 * T), bf16),
+            shape((2, 8 * T, T), bf16), shape((8 * T, T), f32), shape((8, T), f32), shape((8 * T, T), bf16),
+            shape((4, 8 * T, T), bf16), shape((T, 4 * T), bf16),
         ],
         [], 400_000_000, 6_000_000,
-    )(user_low, own_low, other_low, placed, own_resid, user_mid, acc_mid, far_low, trust_placed)
+    )(user_low, other_low, placed, own_prod, user_mid, acc_mid, far_low, trust_placed)
     home_a = send(friend_a, lambda b, g: (b ^ half_bit, g))
     trust_b, friend_b = call(
         second_half,
         [VM] * 3,
-        [shape((8 * T, 4 * T), bf16), shape((T, 4 * T), bf16)],
+        [shape((4, 8 * T, T), bf16), shape((T, 4 * T), bf16)],
         [], 270_000_000, 3_000_000,
     )(rated_low, far_low, trust_placed)
     home_b = send(friend_b, lambda b, g: (b ^ half_bit, g))
@@ -428,12 +459,20 @@
     )(trust_a, trust_b, far_low, user_rated, acc_rated)
     kept, sent = call(split_sum, [VM, VM], [shape((T, T), f32)] * 2, [], 100_000, 400_000)(own_sum, arrived)
     arrived = send(sent, lambda b, g: (b, g ^ 2))
-    item_out, item_acc_out = call(
-        last_items, [VM] * 3, [shape((T, T), f32), shape((1, T), f32)], [], 1_000_000, 400_000
-    )(kept, arrived, share)
+    friend_out, item_out, item_acc_out, friend_acc_mid = call(
+        first_friends,
+        [VM] * 6,
+        [shape((8 * T, T), f32), shape((T, T), f32), shape((1, T), f32), shape((8, T), f32)],
+        [pltpu.VMEM((4 * T, T), f32), pltpu.VMEM((T, T), f32), pltpu.VMEM((1, T), f32), pltpu.SemaphoreType.DMA((3,))],
+        3_000_000, 1_200_000, out_specs=[HBM, HBM, HBM, VM],
+    )(home_a, friend_factors, friend_acc, kept, arrived, share)
     friend_out, friend_acc_out = call(
-        last_friends, [VM] * 4, [shape((8 * T, T), f32), shape((8, T), f32)], [], 4_000_000, 1_500_000
-    )(home_a, home_b, friend_factors, friend_acc)
+        other_friends,
+        [VM] * 3 + [HBM],
+        [shape((8 * T, T), f32), shape((8, T), f32)],
+        [pltpu.VMEM((4 * T, T), f32), pltpu.VMEM((8, T), f32), pltpu.SemaphoreType.DMA((2,))],
+        2_000_000, 900_000, out_specs=[HBM] * 2, aliases={3: 0},
+    )(home_b, friend_factors, friend_acc_mid, friend_out)
     return (
         user_out,
         user_acc_out.reshape(8 * T),

time: 46.9 us -> 47.9 us (1.021)
  waiting for transfers between devices: 16.5 us -> 17.7 us
    ppermute x10, waiting for transfers between devices: 16.5 us -> 17.7 us  [send(): return lax.ppermute(value, axes, route)]
  transfers between devices with their start and end apart: 10 -> 10, of which waited for: 5 -> 3; matrix products, arithmetic and copies ran while one was open for 0% -> 0% of each run, Pallas kernels for 18% -> 17%
where the time goes in v3:
time: 47.9 us; the launch traced here: 47.1 us
  waiting for transfers between devices  17.7 us (37%)
  starting transfers between devices  14.8 us (31%)
  Pallas kernels  13.1 us (27%)
  between operations  1.45 us (3%)
    ppermute x10, waiting for transfers between devices, send(): return lax.ppermute(value, axes, route)  17.7 us
    ppermute x10, starting transfers between devices, send(): return lax.ppermute(value, axes, route)  14.8 us
    pallas_call x14, Pallas kernels, run(): return inner(*args)  13.1 us
  transfers between devices with their start and end apart: 10, of which 3 were waited for; matrix products, arithmetic and copies ran while one was open for 0% of the time, Pallas kernels for 17%

profile of v3, /device:TPU:1, one launch (start us, length us, event | category | flops | bytes accessed | tf_op | source)
XLA Modules:
  0.0 47.1 jit_solution(9646872666044175992)
XLA Ops:
  0.7 2.5 %shard_map.199 = (f32[128,256]{1,0:T(8,128)S(1)}, f32[128,256]{1,0:T(8,128)S(1)}, bf16[2,1024,128]{2,1,0:T(8,128)(2,1)S(1)}, bf16[2,1024,128]{2,1,0:T(8,128)(2,1)S(1)}) custom-call(s32[2,32]{1,0:T(2,128)} %rows_hbm.3, s32[2,32]{1,0:T(2,128)} %cols_hbm.3, s32[2]{0:T(128)} %bitcast.15, f32[1024,128]{1,0:T(8,128)} %user.1, f32[512,128]{1,0:T(8,128)} %item.3, ...), custom_call_target="tpu_custom_call" | custom-call | flops 270000000 | bytes 3000000 | tf_op jit(solution)/shard_map/pallas_call | solution.py:52
  3.1 3.3 %collective-permute-start = (f32[128,256]{1,0:T(8,128)S(1)}, f32[128,256]{1,0:T(8,128)S(1)}, u32[]{:S(2)}, u32[]{:S(2)}) collective-permute-start(f32[128,256]{1,0:T(8,128)S(1)} %get-tuple-element.43), channel_id=1, source_target_pairs={{0,1},{1,0},{2,3},{3,2},{4,5},{5,4},{6,7},{7,6},{8,9},{9,8},{10,11... | collective-permute-start | bytes 393224 | tf_op jit(solution)/shard_map/ppermute | solution.py:368
  6.5 1.3 %collective-permute-start.4 = (bf16[1024,128]{1,0:T(8,128)(2,1)S(1)}, bf16[1024,128]{1,0:T(8,128)(2,1)S(1)}, u32[]{:S(2)}, u32[]{:S(2)}) collective-permute-start(bf16[1024,128]{1,0:T(8,128)(2,1)S(1)} %shard_map.205), channel_id=1, source_target_pairs={{0,128},{1,129},{2,130},{3,131},{4,132},{5,133},{6,134},{7,135},{8... | collective-permute-start | bytes 786440 | tf_op jit(solution)/shard_map/ppermute | solution.py:368
  7.8 1.7 %collective-permute-start.1 = (bf16[128,256]{1,0:T(8,128)(2,1)S(1)}, bf16[128,256]{1,0:T(8,128)(2,1)S(1)}, u32[]{:S(2)}, u32[]{:S(2)}) collective-permute-start(bf16[128,256]{1,0:T(8,128)(2,1)S(1)} %get-tuple-element.45), channel_id=1, source_target_pairs={{0,2},{1,3},{2,0},{3,1},{4,6},{5,7},{6,4},{7,5},{8,10},{9,11},{10,... | collective-permute-start | bytes 196616 | tf_op jit(solution)/shard_map/ppermute | solution.py:368
  9.5 2.1 %collective-permute-done.1.arrived = bf16[128,256]{1,0:T(8,128)(2,1)S(1)} collective-permute-done((bf16[128,256]{1,0:T(8,128)(2,1)S(1)}, bf16[128,256]{1,0:T(8,128)(2,1)S(1)}, u32[]{:S(2)}, u32[]{:S(2)}) %collective-permute-start.1) | collective-permute-done | bytes 65568 | tf_op jit(solution)/shard_map/ppermute | solution.py:368
  11.6 0.4 shard_map.202
  12.0 1.3 %collective-permute-start.2 = (bf16[256,128]{1,0:T(8,128)(2,1)S(1)}, bf16[256,128]{1,0:T(8,128)(2,1)S(1)}, u32[]{:S(2)}, u32[]{:S(2)}) collective-permute-start(bf16[256,128]{1,0:T(8,128)(2,1)S(1)} %get-tuple-element.46), channel_id=1, source_target_pairs={{0,4},{1,5},{2,6},{3,7},{4,8},{5,9},{6,10},{7,11},{8,12},{9,13},{1... | collective-permute-start | bytes 196616 | tf_op jit(solution)/shard_map/ppermute | solution.py:368
  13.2 8.7 %collective-permute-done.2.own_low = bf16[256,128]{1,0:T(8,128)(2,1)S(1)} collective-permute-done((bf16[256,128]{1,0:T(8,128)(2,1)S(1)}, bf16[256,128]{1,0:T(8,128)(2,1)S(1)}, u32[]{:S(2)}, u32[]{:S(2)}) %collective-permute-start.2) | collective-permute-done | bytes 65568 | tf_op jit(solution)/shard_map/ppermute | solution.py:368
  21.9 2.7 %collective-permute-start.3 = (bf16[256,128]{1,0:T(8,128)(2,1)S(1)}, bf16[256,128]{1,0:T(8,128)(2,1)S(1)}, u32[]{:S(2)}, u32[]{:S(2)}) collective-permute-start(bf16[256,128]{1,0:T(8,128)(2,1)S(1)} %collective-permute-done.2.own_low), channel_id=1, source_target_pairs={{0,1},{1,0},{2,3},{3,2},{4,5},{5,4},{6,7},{7,6},{8,9},{9,8},{10,11... | collective-permute-start | bytes 196616 | tf_op jit(solution)/shard_map/ppermute | solution.py:368
  25.3 2.6 %shard_map.203 = (f32[4,1024,128]{2,1,0:T(8,128)S(1)}, f32[8,1024,128]{2,1,0:T(8,128)S(1)}) custom-call(s32[2,32]{1,0:T(2,128)} %rows_hbm.3, s32[2,32]{1,0:T(2,128)} %cols_hbm.3, s32[2]{0:T(128)} %bitcast.16, s32[48]{0:T(128)} %trust_rows_hbm.1, s32[48]{0:T(128)} %trust_cols_hbm.1, s32[1]{0:T(128)S(6)} %copy.24.trust_count, ...), custom_call_target="tpu_custom_call" | custom-call | flops 20000000 | bytes 6000000 | tf_op jit(solution)/shard_map/pallas_call | solution.py:52
  27.9 0.5 %shard_map.200 = (f32[1024,128]{1,0:T(8,128)S(1)}, f32[8,128]{1,0:T(8,128)S(1)}, bf16[1024,128]{1,0:T(8,128)(2,1)S(1)}) custom-call(bf16[2,1024,128]{2,1,0:T(8,128)(2,1)S(1)} %get-tuple-element.39.own_resid, bf16[2,1024,128]{2,1,0:T(8,128)(2,1)S(1)} %get-tuple-element.40.other_resid, f32[1024,128]{1,0:T(8,128)S(1)} %copy-done.2, f32[512,128]{1,0:T(8,128)S(1)} %copy-done.1, ...), custom_call_target="tpu_custom_call" | custom-call | flops 140000000 | bytes 3000000 | tf_op jit(solution)/shard_map/pallas_call | solution.py:52
  28.5 1.3 %shard_map.204 = (bf16[2,1024,128]{2,1,0:T(8,128)(2,1)}, f32[128,256]{1,0:T(8,128)S(1)}, f32[1024,128]{1,0:T(8,128)S(1)}) custom-call(bf16[1024,128]{1,0:T(8,128)(2,1)S(1)} %get-tuple-element.41.user_low, bf16[256,128]{1,0:T(8,128)(2,1)S(1)} %collective-permute-done.2.own_low, f32[4,1024,128]{2,1,0:T(8,128)S(1)} %get-tuple-element.47.placed), custom_call_target="tpu_custom_call" | custom-call | flops 200000000 | bytes 1500000 | tf_op jit(solution)/shard_map/pallas_call | solution.py:52
  29.7 1.2 %shard_map.206 = (bf16[2,1024,128]{2,1,0:T(8,128)(2,1)S(1)}, f32[1024,128]{1,0:T(8,128)S(1)}, f32[8,128]{1,0:T(8,128)S(1)}, bf16[1024,128]{1,0:T(8,128)(2,1)S(1)...) custom-call(bf16[1024,128]{1,0:T(8,128)(2,1)S(1)} %get-tuple-element.41.user_low, ...), custom_call_target="tpu_custom_call" | custom-call | flops 400000000 | bytes 6000000 | tf_op jit(solution)/shard_map/pallas_call | solution.py:52
  30.9 0.3 shard_map.209
  31.2 0.1 collective-permute-start.7
  31.3 1.6 %collective-permute-start.6 = (bf16[128,512]{1,0:T(8,128)(2,1)S(1)}, bf16[128,512]{1,0:T(8,128)(2,1)S(1)}, u32[]{:S(2)}, u32[]{:S(2)}) collective-permute-start(bf16[128,512]{1,0:T(8,128)(2,1)S(1)} %get-tuple-element.60), channel_id=1, source_target_pairs={{0,128},{1,129},{2,130},{3,131},{4,132},{5,133},{6,134},{7,135},{8... | collective-permute-start | bytes 393224 | tf_op jit(solution)/shard_map/ppermute | solution.py:368
  32.9 0.7 %shard_map.207 = (bf16[4,1024,128]{2,1,0:T(8,128)(2,1)S(1)}, bf16[128,512]{1,0:T(8,128)(2,1)S(1)}) custom-call(bf16[1024,128]{1,0:T(8,128)(2,1)S(1)} %get-tuple-element.53.rated_low, bf16[1024,128]{1,0:T(8,128)(2,1)S(1)} %collective-permute-done.4.far_low, f32[8,1024,128]{2,1,0:T(8,128)S(1)} %get-tuple-element.51.trust_placed), custom_call_target="tpu_custom_call" | custom-call | flops 270000000 | bytes 3000000 | tf_op jit(solution)/shard_map/pallas_call | solution.py:52
  33.6 0.0 copy-start.4
  33.6 1.6 %collective-permute-start.5 = (bf16[128,512]{1,0:T(8,128)(2,1)S(1)}, bf16[128,512]{1,0:T(8,128)(2,1)S(1)}, u32[]{:S(2)}, u32[]{:S(2)}) collective-permute-start(bf16[128,512]{1,0:T(8,128)(2,1)S(1)} %get-tuple-element.59), channel_id=1, source_target_pairs={{0,128},{1,129},{2,130},{3,131},{4,132},{5,133},{6,134},{7,135},{8... | collective-permute-start | bytes 393224 | tf_op jit(solution)/shard_map/ppermute | solution.py:368
  35.2 1.3 %collective-permute-start.8 = (f32[128,128]{1,0:T(8,128)S(1)}, f32[128,128]{1,0:T(8,128)S(1)}, u32[]{:S(2)}, u32[]{:S(2)}) collective-permute-start(f32[128,128]{1,0:T(8,128)S(1)} %get-tuple-element.64), channel_id=1, source_target_pairs={{0,2},{1,3},{2,0},{3,1},{4,6},{5,7},{6,4},{7,5},{8,10},{9,11},{10,... | collective-permute-start | bytes 196616 | tf_op jit(solution)/shard_map/ppermute | solution.py:368
  36.5 1.6 %shard_map.208 = (f32[1024,128]{1,0:T(8,128)}, f32[8,128]{1,0:T(8,128)}) custom-call(bf16[4,1024,128]{2,1,0:T(8,128)(2,1)S(1)} %get-tuple-element.52.first_resid, bf16[4,1024,128]{2,1,0:T(8,128)(2,1)S(1)} %get-tuple-element.54.second_resid, bf16[1024,128]{1,0:T(8,128)(2,1)S(1)} %collective-permute-done.4.far_low, ...), custom_call_target="tpu_custom_call" | custom-call | flops 270000000 | bytes 4000000 | tf_op jit(solution)/shard_map/pallas_call | solution.py:52
  38.1 6.9 %collective-permute-done.9.share = f32[136,128]{1,0:T(8,128)S(1)} collective-permute-done((f32[136,128]{1,0:T(8,128)S(1)}, f32[136,128]{1,0:T(8,128)S(1)}, u32[]{:S(2)}, u32[]{:S(2)}) %collective-permute-start.9) | collective-permute-done | bytes 69664 | tf_op jit(solution)/shard_map/ppermute | solution.py:368
  45.1 1.0 %shard_map.211 = (f32[1024,128]{1,0:T(8,128)}, f32[128,128]{1,0:T(8,128)}, f32[1,128]{1,0:T(1,128)}, f32[8,128]{1,0:T(8,128)S(1)}) custom-call(bf16[128,512]{1,0:T(8,128)(2,1)S(1)} %collective-permute-done.6.home, f32[1024,128]{1,0:T(8,128)S(1)} %copy-done, f32[8,128]{1,0:T(8,128)S(1)} %bitcast.10, f32[128,128]{1,0:T(8,128)S(1)} %get-tuple-element.63.kept, ...), custom_call_target="tpu_custom_call" | custom-call | flops 3000000 | bytes 1200000 | tf_op jit(solution)/shard_map/pallas_call | solution.py:52
  46.1 1.0 %shard_map.212 = (f32[1024,128]{1,0:T(8,128)}, f32[8,128]{1,0:T(8,128)}) custom-call(bf16[128,512]{1,0:T(8,128)(2,1)S(1)} %collective-permute-done.5.home, f32[1024,128]{1,0:T(8,128)S(1)} %copy-done, f32[8,128]{1,0:T(8,128)S(1)} %get-tuple-element.66.acc, f32[1024,128]{1,0:T(8,128)} %get-tuple-element.67.earlier), custom_call_target="tpu_custom_call", output_to_operand_aliasing={{0}: (3, {})} | custom-call | flops 2000000 | bytes 900000 | tf_op jit(solution)/shard_map/pallas_call | solution.py:52
  (22 shorter events, 0.1 us)
Async XLA Ops:
  0.6 5.8 %copy-start = (f32[1024,128]{1,0:T(8,128)S(1)}, f32[1024,128]{1,0:T(8,128)}, u32[]{:S(2)}) copy-start(f32[1024,128]{1,0:T(8,128)} %friend.5) | copy-start | bytes 1572868
  0.6 10.9 %copy-start.1 = (f32[512,128]{1,0:T(8,128)S(1)}, f32[512,128]{1,0:T(8,128)}, u32[]{:S(2)}) copy-start(f32[512,128]{1,0:T(8,128)} %item.3) | copy-start | bytes 786436
  0.7 10.9 %copy-start.5 = (f32[512]{0:T(512)S(1)}, f32[512]{0:T(512)}, u32[]{:S(2)}) copy-start(f32[512]{0:T(512)} %param.21) | copy-start | bytes 6148
  3.1 4.6 %collective-permute-start = (f32[128,256]{1,0:T(8,128)S(1)}, f32[128,256]{1,0:T(8,128)S(1)}, u32[]{:S(2)}, u32[]{:S(2)}) collective-permute-start(f32[128,256]{1,0:T(8,128)S(1)} %get-tuple-element.43), channel_id=1, source_target_pairs={{0,1},{1,0},{2,3},{3,2},{4,5},{5,4},{6,7},{7,6},{8,9},{9,8},{10,11... | collective-permute-start | bytes 393224 | tf_op jit(solution)/shard_map/ppermute | solution.py:368
  6.5 23.2 %collective-permute-start.4 = (bf16[1024,128]{1,0:T(8,128)(2,1)S(1)}, bf16[1024,128]{1,0:T(8,128)(2,1)S(1)}, u32[]{:S(2)}, u32[]{:S(2)}) collective-permute-start(bf16[1024,128]{1,0:T(8,128)(2,1)S(1)} %shard_map.205), channel_id=1, source_target_pairs={{0,128},{1,129},{2,130},{3,131},{4,132},{5,133},{6,134},{7,135},{8... | collective-permute-start | bytes 786440 | tf_op jit(solution)/shard_map/ppermute | solution.py:368
  7.8 3.8 %collective-permute-start.1 = (bf16[128,256]{1,0:T(8,128)(2,1)S(1)}, bf16[128,256]{1,0:T(8,128)(2,1)S(1)}, u32[]{:S(2)}, u32[]{:S(2)}) collective-permute-start(bf16[128,256]{1,0:T(8,128)(2,1)S(1)} %get-tuple-element.45), channel_id=1, source_target_pairs={{0,2},{1,3},{2,0},{3,1},{4,6},{5,7},{6,4},{7,5},{8,10},{9,11},{10,... | collective-permute-start | bytes 196616 | tf_op jit(solution)/shard_map/ppermute | solution.py:368
  12.0 10.0 %collective-permute-start.2 = (bf16[256,128]{1,0:T(8,128)(2,1)S(1)}, bf16[256,128]{1,0:T(8,128)(2,1)S(1)}, u32[]{:S(2)}, u32[]{:S(2)}) collective-permute-start(bf16[256,128]{1,0:T(8,128)(2,1)S(1)} %get-tuple-element.46), channel_id=1, source_target_pairs={{0,4},{1,5},{2,6},{3,7},{4,8},{5,9},{6,10},{7,11},{8,12},{9,13},{1... | collective-permute-start | bytes 196616 | tf_op jit(solution)/shard_map/ppermute | solution.py:368
  21.9 7.8 %collective-permute-start.3 = (bf16[256,128]{1,0:T(8,128)(2,1)S(1)}, bf16[256,128]{1,0:T(8,128)(2,1)S(1)}, u32[]{:S(2)}, u32[]{:S(2)}) collective-permute-start(bf16[256,128]{1,0:T(8,128)(2,1)S(1)} %collective-permute-done.2.own_low), channel_id=1, source_target_pairs={{0,1},{1,0},{2,3},{3,2},{4,5},{5,4},{6,7},{7,6},{8,9},{9,8},{10,11... | collective-permute-start | bytes 196616 | tf_op jit(solution)/shard_map/ppermute | solution.py:368
  25.3 2.6 %copy-start.2 = (f32[1024,128]{1,0:T(8,128)S(1)}, f32[1024,128]{1,0:T(8,128)}, u32[]{:S(2)}) copy-start(f32[1024,128]{1,0:T(8,128)} %user.1) | copy-start | bytes 1572868
  25.3 2.6 %copy-start.3 = (f32[1024]{0:T(1024)S(1)}, f32[1024]{0:T(1024)}, u32[]{:S(2)}) copy-start(f32[1024]{0:T(1024)} %param.17) | copy-start | bytes 12292
  31.2 4.0 %collective-permute-start.7 = (f32[128,256]{1,0:T(8,128)S(1)}, f32[128,256]{1,0:T(8,128)S(1)}, u32[]{:S(2)}, u32[]{:S(2)}) collective-permute-start(f32[128,256]{1,0:T(8,128)S(1)} %shard_map.209), channel_id=1, source_target_pairs={{0,1},{1,0},{2,3},{3,2},{4,5},{5,4},{6,7},{7,6},{8,9},{9,8},{10,11... | collective-permute-start | bytes 393224 | tf_op jit(solution)/shard_map/ppermute | solution.py:368
  31.3 13.7 %collective-permute-start.6 = (bf16[128,512]{1,0:T(8,128)(2,1)S(1)}, bf16[128,512]{1,0:T(8,128)(2,1)S(1)}, u32[]{:S(2)}, u32[]{:S(2)}) collective-permute-start(bf16[128,512]{1,0:T(8,128)(2,1)S(1)} %get-tuple-element.60), channel_id=1, source_target_pairs={{0,128},{1,129},{2,130},{3,131},{4,132},{5,133},{6,134},{7,135},{8... | collective-permute-start | bytes 393224 | tf_op jit(solution)/shard_map/ppermute | solution.py:368
  33.6 11.5 %copy-start.4 = (f32[1024]{0:T(1024)S(1)}, f32[1024]{0:T(1024)}, u32[]{:S(2)}) copy-start(f32[1024]{0:T(1024)} %param.19) | copy-start | bytes 12292
  33.6 12.5 %collective-permute-start.5 = (bf16[128,512]{1,0:T(8,128)(2,1)S(1)}, bf16[128,512]{1,0:T(8,128)(2,1)S(1)}, u32[]{:S(2)}, u32[]{:S(2)}) collective-permute-start(bf16[128,512]{1,0:T(8,128)(2,1)S(1)} %get-tuple-element.59), channel_id=1, source_target_pairs={{0,128},{1,129},{2,130},{3,131},{4,132},{5,133},{6,134},{7,135},{8... | collective-permute-start | bytes 393224 | tf_op jit(solution)/shard_map/ppermute | solution.py:368
  35.2 9.9 %collective-permute-start.9 = (f32[136,128]{1,0:T(8,128)S(1)}, f32[136,128]{1,0:T(8,128)S(1)}, u32[]{:S(2)}, u32[]{:S(2)}) collective-permute-start(f32[136,128]{1,0:T(8,128)S(1)} %get-tuple-element.65), channel_id=1, source_target_pairs={{0,4},{1,5},{2,6},{3,7},{4,8},{5,9},{6,10},{7,11},{8,12},{9,13},{1... | collective-permute-start | bytes 208904 | tf_op jit(solution)/shard_map/ppermute | solution.py:368
  35.2 9.8 %collective-permute-start.8 = (f32[128,128]{1,0:T(8,128)S(1)}, f32[128,128]{1,0:T(8,128)S(1)}, u32[]{:S(2)}, u32[]{:S(2)}) collective-permute-start(f32[128,128]{1,0:T(8,128)S(1)} %get-tuple-element.64), channel_id=1, source_target_pairs={{0,2},{1,3},{2,0},{3,1},{4,6},{5,7},{6,4},{7,5},{8,10},{9,11},{10,... | collective-permute-start | bytes 196616 | tf_op jit(solution)/shard_map/ppermute | solution.py:368
